TPU v7x, 32 devices: a whole 2x2x4 slice. The times are simulated.
32 devices in a mesh: space: 8 (over z, y), tm: 4 (over x, core).
Axes of the slice: x: 2, y: 2, z: 4, core: 2. Of those that a mesh axis runs over, the one named last changes fastest.
Arguments:
- view_tiles: bfloat16 [4, 512, 2, 8, 256], P('tm', 'space'), may hold values from -6 to 6
- tile_routes: int32 [4, 512, 2], P('tm', 'space'), may hold values from 0 to 7, all different within a row; in each aligned block of 64 rows (0 to 63, 64 to 127, ..., all dimensions but the last counted through in order) at most 32 rows name the same one
- blend_weights: bfloat16 [4, 512, 2], P('tm', 'space'), may hold values from 0.5 to 4
- tile_view: int32 [4, 512], P('tm', 'space'), may hold values from 0 to 4
- view_shift: int32 [5], replicated, may hold values from -3 to 3
- view_frac: bfloat16 [5], replicated, may hold values from 0.099609375 to 0.8984375
- atlas_image: bfloat16 [16, 8, 256], P('space'), may hold values from -6 to 6
- displacement: float32 [4, 3, 16, 8, 256], P('tm', None, 'space'), may hold values from -4 to 4
Outputs:
- joined_image: float32 [4, 16, 8, 256], P('tm', 'space')
- updated_field: float32 [4, 3, 16, 8, 256], P('tm', None, 'space')
Inputs may be any that keep to these rules, and one draw needn't show every extreme that they name: `tile_routes`: each tile names 2 different bricks. Among the tiles of one device (aligned blocks of 64 rows, timepoints in order) no brick is named more than 32 times, a bound that some block reaches.
All inputs are finite; a program needn't handle non-finite values.
Results may differ from a plain program's by a relative error of at most 0.0003.
Values may be sent and summed in bfloat16 or wider, within the bound.
No kernel may reach another device: no remote copies, remote signals or barrier semaphores. Data moves between devices by JAX's collectives and lax.ppermute only.
A program may use at most 64 MiB of HBM per device.

v0:
```python
import jax
import jax.numpy as jnp
from jax import lax
from jax.sharding import PartitionSpec as P

TOP = 2
TILES_DEV = 64


SHIFT_LOW = -3
SHIFT_HIGH = 4
KAPPA = 0.25


def extended(cells, sides, width):
    for axis, dim in sides:
        count = lax.axis_size(axis)
        ends = count - 1
        head = lax.slice_in_dim(cells, 0, width, axis=dim)
        tail = lax.slice_in_dim(cells, cells.shape[dim] - width, cells.shape[dim], axis=dim)
        cells = jnp.concatenate(
            [
                lax.ppermute(tail, axis, [(i, (i + 1) % count) for i in range(ends)]),
                cells,
                lax.ppermute(head, axis, [((i + 1) % count, i) for i in range(ends)]),
            ],
            axis=dim,
        )
    return cells


def shifted(values, offset):
    width = values.shape[-1]
    padding = [(0, 0)] * (values.ndim - 1) + [(4, 4)]
    padded = jnp.pad(values, padding)
    return padded[..., 4 + offset : 4 + offset + width]


def warp_lines(values, shift_by, fraction):
    shift_by = shift_by[..., None, None, None]
    fraction = fraction[..., None, None, None]
    summed = jnp.zeros(values.shape, jnp.float32)
    for offset in range(SHIFT_LOW, SHIFT_HIGH + 1):
        factor = jnp.where(shift_by == offset, 1.0 - fraction, 0.0) + jnp.where(
            shift_by + 1 == offset, fraction, 0.0
        )
        summed = summed + factor * shifted(values, offset)
    return summed


def blend_items(pieces):
    voxels, details = pieces
    details_wide = details.astype(jnp.float32)
    weight = details_wide[..., 0]
    warped = warp_lines(voxels.astype(jnp.float32), details_wide[..., 1], details_wide[..., 2])
    return (weight[..., None, None, None] * warped, weight)


def shards(
    view_tiles,
    tile_routes,
    blend_weights,
    tile_view,
    view_shift,
    view_frac,
    atlas_image,
    displacement,
):
    nspace = lax.axis_size("space")
    capacity = max(2, 2 * TILES_DEV * TOP // nspace)
    send_count = TILES_DEV * TOP
    slot_count = nspace * capacity
    target = tile_routes[0].reshape(send_count)
    onehot = (target[:, None] == jnp.arange(nspace, dtype=jnp.int32)[None, :]).astype(jnp.int32)
    earlier = jnp.cumsum(onehot, axis=0) - onehot
    position = jnp.sum(onehot * earlier, axis=1)
    slot_index = target * capacity + position
    matches = slot_index[None, :] == jnp.arange(slot_count, dtype=jnp.int32)[:, None]
    filled = jnp.any(matches, axis=1)
    source = jnp.sum(
        jnp.where(matches, jnp.arange(send_count, dtype=jnp.int32)[None, :], 0), axis=1
    )
    tile_of = source // TOP
    weight_flat = blend_weights[0].reshape(send_count)
    slot_weight = jnp.where(filled, weight_flat[source], jnp.zeros((), jnp.bfloat16))
    view_of = tile_view[0]
    shape_tail = view_tiles.shape[2:]
    raw_data = jnp.where(
        filled[:, None, None, None], view_tiles[0][tile_of], jnp.zeros((), jnp.bfloat16)
    ).reshape((nspace, capacity) + shape_tail)
    shift_slot = view_shift[view_of][tile_of].astype(jnp.bfloat16)
    frac_slot = view_frac[view_of][tile_of]
    slot_info = jnp.stack([slot_weight, shift_slot, frac_slot], axis=1).reshape(nspace, capacity, 3)
    weighted, weight_parts = blend_items(
        (
            lax.all_to_all(raw_data, "space", split_axis=0, concat_axis=0, tiled=True),
            lax.all_to_all(slot_info, "space", split_axis=0, concat_axis=0, tiled=True),
        )
    )
    numerator = jnp.sum(weighted, axis=(0, 1))
    weight_sum = jnp.sum(weight_parts)
    joined = numerator / (1.0 + weight_sum)
    mismatch = joined - atlas_image.astype(jnp.float32)
    face_cells = extended(joined, (("space", 0),), 1)
    grad_x = (face_cells[2:] - face_cells[:-2]) * 0.5
    padded = jnp.pad(joined, ((0, 0), (1, 1), (1, 1)))
    grad_y = (padded[:, 2:, 1:-1] - padded[:, :-2, 1:-1]) * 0.5
    grad_z = (padded[:, 1:-1, 2:] - padded[:, 1:-1, :-2]) * 0.5
    scaled = mismatch / (
        grad_x * grad_x + grad_y * grad_y + grad_z * grad_z + mismatch * mismatch + 1.0
    )
    forces = jnp.stack([grad_x * scaled, grad_y * scaled, grad_z * scaled])
    stepped = displacement[0] + forces
    time_rims = extended(stepped[None], (("tm", 0),), 1)
    before_time = time_rims[0]
    after_time = time_rims[2]
    updated = stepped + KAPPA * (before_time - 2.0 * stepped + after_time)
    return (joined[None], updated[None])


def solution(mesh):
    in_specs = (
        P("tm", "space", None, None, None),
        P("tm", "space", None),
        P("tm", "space", None),
        P("tm", "space"),
        P(),
        P(),
        P("space", None, None),
        P("tm", None, "space", None, None),
    )
    out_specs = (P("tm", "space", None, None), P("tm", None, "space", None, None))
    return jax.shard_map(shards, mesh=mesh, in_specs=in_specs, out_specs=out_specs, check_vma=False)
```

profile of v0, /device:TPU:0, one launch (start us, length us, event | category | flops | bytes accessed | tf_op | source)
XLA Modules:
  0.0 111.4 jit_solution(10721143964574499156)
XLA Ops:
  0.6 0.0 copy-start
  0.6 0.8 copy.19
  1.5 0.1 reshape_squeeze.6
  1.6 0.1 fusion.17
  1.7 0.2 reduce_window_sum.11
  1.9 0.2 select_reduce_fusion.1
  2.1 0.1 select_reduce_fusion
  2.2 0.1 fusion.16
  2.3 1.5 %fusion.36 = (bf16[1]{0:T(256)(128)(2,1)}, bf16[1]{0:T(256)(128)(2,1)}, bf16[1]{0:T(256)(128)(2,1)}, bf16[1]{0:T(256)(128)(2,1)}, bf16[1]{0:T(256)(128)(2,1)}) fusion(bf16[5]{0:T(256)(128)(2,1)} %param.13), kind=kLoop, calls=%fused_computation.104 | loop fusion | bytes 20 | tf_op jit(solution)/shard_map/gather | solution.py:92
  3.8 3.8 %fusion.32 = bf16[64]{0:T(256)(128)(2,1)S(1)} fusion(bf16[]{:T(256)} %bitcast.10, bf16[]{:T(256)} %bitcast.11, bf16[]{:T(256)} %bitcast.12, bf16[]{:T(256)} %bitcast.14, bf16[]{:T(256)} %bitcast.13, s32[1,64]{1,0:T(1,128)} %param.11), kind=kLoop, calls=%fused_computation.97 | loop fusion | flops 704 | bytes 394 | tf_op jit(solution)/shard_map/gather | solution.py:92
  7.6 1.9 %gather_fusion.2 = bf16[256]{0:T(256)(128)(2,1)S(1)} fusion(bf16[64]{0:T(256)(128)(2,1)S(1)} %fusion.32, s32[1024]{0:T(1024)S(1)} %pad_clamp_fusion), kind=kCustom, calls=%fused_computation.2 | custom fusion | bytes 2048 | tf_op jit(solution)/shard_map/gather | solution.py:92
  9.5 0.1 stack.20
  9.6 1.5 %fusion.35 = (s32[1]{0:T(128)}, s32[1]{0:T(128)}, s32[1]{0:T(128)}, s32[1]{0:T(128)}, s32[1]{0:T(128)}) fusion(s32[5]{0:T(128)} %param.12), kind=kLoop, calls=%fused_computation.103 | loop fusion | bytes 40 | tf_op jit(solution)/shard_map/gather | solution.py:91
  11.1 3.8 %fusion.33 = s32[64]{0:T(128)S(1)} fusion(s32[]{:T(128)} %bitcast.3, s32[]{:T(128)} %bitcast.4, s32[]{:T(128)} %bitcast.5, s32[]{:T(128)} %bitcast.7, s32[]{:T(128)} %bitcast.6, s32[1,64]{1,0:T(1,128)} %param.11), kind=kLoop, calls=%fused_computation.98 | loop fusion | flops 704 | bytes 532 | tf_op jit(solution)/shard_map/gather | solution.py:91
  14.9 1.9 %gather_fusion.1 = s32[256]{0:T(256)S(1)} fusion(s32[64]{0:T(128)S(1)} %fusion.33, s32[1024]{0:T(1024)S(1)} %pad_clamp_fusion), kind=kCustom, calls=%fused_computation.1 | custom fusion | bytes 3072 | tf_op jit(solution)/shard_map/gather | solution.py:91
  16.8 0.1 convert_element_type.39
  16.8 0.8 copy.20
  17.6 0.1 reshape_squeeze.7
  17.8 1.9 %gather_fusion = bf16[256]{0:T(256)(128)(2,1)S(1)} fusion(bf16[128]{0:T(256)(128)(2,1)S(1)} %reshape_squeeze.7, s32[1024]{0:T(1024)S(1)} %pad_clamp_fusion.1), kind=kCustom, calls=%fused_computation | custom fusion | bytes 2048 | tf_op jit(solution)/shard_map/gather | solution.py:85
  19.7 0.1 select_n.249
  19.8 0.6 copy.21
  20.4 7.3 %all-to-all-start = ((bf16[8,32,3]{1,2,0:T(4,128)(2,1)}), bf16[8,32,3]{1,2,0:T(4,128)(2,1)S(1)}, u32[]{:S(2)}, u32[]{:S(2)}) async-start(bf16[8,32,3]{1,2,0:T(4,128)(2,1)} %copy.21), calls=%async_computation | async-start | bytes 16384 | tf_op jit(solution)/shard_map/all_to_all | solution.py:97
  27.7 0.1 broadcast_in_dim.67
  27.8 0.0 copy-done
  27.8 0.8 gather_fusion.3
  28.5 1.6 %broadcast_select_fusion = bf16[8,32,2,8,256]{4,3,2,1,0:T(8,128)(2,1)} fusion(bf16[8,32,2,8,256]{4,3,2,1,0:T(8,128)(2,1)S(1)} %bitcast.43, pred[8,32]{1,0:T(8,128)(4,1)S(1)} %broadcast_in_dim.67), kind=kLoop, calls=%fused_computation.27 | loop fusion | flops 1048576 | bytes 4194560 | tf_op jit(solution)/shard_map/jit(_where)/select_n | solution.py:88
  30.1 4.1 %all-to-all-done = bf16[8,32,3]{1,2,0:T(4,128)(2,1)S(1)} async-done(((bf16[8,32,3]{1,2,0:T(4,128)(2,1)}), bf16[8,32,3]{1,2,0:T(4,128)(2,1)S(1)}, u32[]{:S(2)}, u32[]{:S(2)}) %all-to-all-start) | async-done | bytes 1568 | tf_op jit(solution)/shard_map/all_to_all | solution.py:97
  34.2 3.6 %all-to-all-start.1 = ((bf16[8,32,2,8,256]{4,3,2,1,0:T(8,128)(2,1)}), bf16[8,32,2,8,256]{4,3,2,1,0:T(8,128)(2,1)S(1)}, u32[]{:S(2)}, u32[]{:S(2)}) async-start(bf16[8,32,2,8,256]{4,3,2,1,0:T(8,128)(2,1)} %broadcast_select_fusion), calls=%async_computation.1 | async-start | bytes 4194304 | tf_op jit(solution)/shard_map/all_to_all | solution.py:96
  37.8 0.7 slice_reduce_fusion
  39.1 0.0 copy-start.2
  39.1 0.0 copy-start.1
  39.2 45.7 %all-to-all-done.1 = bf16[8,32,2,8,256]{4,3,2,1,0:T(8,128)(2,1)S(1)} async-done(((bf16[8,32,2,8,256]{4,3,2,1,0:T(8,128)(2,1)}), bf16[8,32,2,8,256]{4,3,2,1,0:T(8,128)(2,1)S(1)}, u32[]{:S(2)}, u32[]{:S(2)}) %all-to-all-start.1) | async-done | bytes 2097184 | tf_op jit(solution)/shard_map/all_to_all | solution.py:96
  84.8 0.6 convert_element_type.41
  85.4 11.1 %fusion.15 = f32[2,8,256]{2,1,0:T(8,128)S(1)} fusion(f32[8,32,2,8,256]{4,3,2,1,0:T(8,128)S(1)} %convert_element_type.41, f32[8,32]{1,0:T(8,128)S(1)} %bitcast.49, f32[8,32]{1,0:T(8,128)S(1)} %bitcast.48, f32[8,32]{1,0:T(8,128)S(1)} %bitcast.47, f32[8,32]{1,0:T(8,128)S(1)} %bitcast.46, f32[8,32]{1,0:T(8,128)S(1)} %bitcast.45, f32[8,32]{1,0:T(8,128)S(1)} %bitcast.44, ...), kind=kLoop, calls=%fused_computation.26 | loop fusion | flops 17821696 | bytes 4219904 | tf_op jit(solution)/shard_map/reduce_sum | solution.py:100
  96.5 3.4 %collective-permute-start.1 = (f32[1,8,256]{2,1,0:T(8,128)S(1)}, f32[1,8,256]{2,1,0:T(8,128)S(1)}, u32[]{:S(2)}, u32[]{:S(2)}) collective-permute-start(f32[1,8,256]{2,1,0:T(8,128)S(1)} %get-tuple-element.7), channel_id=1, source_target_pairs={{0,4},{4,8},{8,12},{12,16},{16,20},{20,24},{24,28},{1,5},{5,9},{9,... | collective-permute-start | bytes 24584 | tf_op jit(solution)/shard_map/ppermute | solution.py:23
  99.9 1.3 %collective-permute-start = (f32[1,8,256]{2,1,0:T(8,128)S(1)}, f32[1,8,256]{2,1,0:T(8,128)S(1)}, u32[]{:S(2)}, u32[]{:S(2)}) collective-permute-start(f32[1,8,256]{2,1,0:T(8,128)S(1)} %get-tuple-element.6), channel_id=1, source_target_pairs={{4,0},{8,4},{12,8},{16,12},{20,16},{24,20},{28,24},{5,1},{9,5},{13... | collective-permute-start | bytes 24584 | tf_op jit(solution)/shard_map/ppermute | solution.py:25
  101.2 0.0 collective-permute-done.1
  101.2 4.2 %collective-permute-done = f32[1,8,256]{2,1,0:T(8,128)S(1)} collective-permute-done((f32[1,8,256]{2,1,0:T(8,128)S(1)}, f32[1,8,256]{2,1,0:T(8,128)S(1)}, u32[]{:S(2)}, u32[]{:S(2)}) %collective-permute-start) | collective-permute-done | bytes 8224 | tf_op jit(solution)/shard_map/ppermute | solution.py:25
  105.4 0.0 copy-done.2
  105.4 0.1 multiply_bitcast_fusion.2
  105.5 0.1 multiply_bitcast_fusion.1
  105.6 0.0 copy-done.1
  105.6 1.3 %collective-permute-start.3 = (f32[1,3,2,8,256]{4,3,2,1,0:T(8,128)S(1)}, f32[1,3,2,8,256]{4,3,2,1,0:T(8,128)S(1)}, u32[]{:S(2)}, u32[]{:S(2)}) collective-permute-start(f32[1,3,2,8,256]{4,3,2,1,0:T(8,128)S(1)} %maximum_add_fusion), channel_id=1, source_target_pairs={{1,0},{2,1},{3,2},{5,4},{6,5},{7,6},{9,8},{10,9},{11,10},{13,12},{... | collective-permute-start | bytes 147464 | tf_op jit(solution)/shard_map/ppermute | solution.py:25
  106.9 3.0 %collective-permute-start.2 = (f32[1,3,2,8,256]{4,3,2,1,0:T(8,128)S(1)}, f32[1,3,2,8,256]{4,3,2,1,0:T(8,128)S(1)}, u32[]{:S(2)}, u32[]{:S(2)}) collective-permute-start(f32[1,3,2,8,256]{4,3,2,1,0:T(8,128)S(1)} %maximum_add_fusion), channel_id=1, source_target_pairs={{0,1},{1,2},{2,3},{4,5},{5,6},{6,7},{8,9},{9,10},{10,11},{12,13},{... | collective-permute-start | bytes 147464 | tf_op jit(solution)/shard_map/ppermute | solution.py:23
  109.9 0.6 fusion.37
  110.6 0.0 collective-permute-done.3
  110.6 0.2 collective-permute-done.2
  110.8 0.6 multiply_add_fusion
  (12 shorter events, 0.1 us)
Async XLA Ops:
  0.6 27.1 %copy-start = (bf16[1,64,2,8,256]{4,3,2,1,0:T(8,128)(2,1)S(1)}, bf16[1,64,2,8,256]{4,3,2,1,0:T(8,128)(2,1)}, u32[]{:S(2)}) copy-start(bf16[1,64,2,8,256]{4,3,2,1,0:T(8,128)(2,1)} %param.8) | copy-start | bytes 1572868
  20.4 13.8 %all-to-all-start = ((bf16[8,32,3]{1,2,0:T(4,128)(2,1)}), bf16[8,32,3]{1,2,0:T(4,128)(2,1)S(1)}, u32[]{:S(2)}, u32[]{:S(2)}) async-start(bf16[8,32,3]{1,2,0:T(4,128)(2,1)} %copy.21), calls=%async_computation | async-start | bytes 16384 | tf_op jit(solution)/shard_map/all_to_all | solution.py:97
  34.2 50.6 %all-to-all-start.1 = ((bf16[8,32,2,8,256]{4,3,2,1,0:T(8,128)(2,1)}), bf16[8,32,2,8,256]{4,3,2,1,0:T(8,128)(2,1)S(1)}, u32[]{:S(2)}, u32[]{:S(2)}) async-start(bf16[8,32,2,8,256]{4,3,2,1,0:T(8,128)(2,1)} %broadcast_select_fusion), calls=%async_computation.1 | async-start | bytes 4194304 | tf_op jit(solution)/shard_map/all_to_all | solution.py:96
  39.1 66.3 %copy-start.2 = (bf16[2,8,256]{2,1,0:T(8,128)(2,1)S(1)}, bf16[2,8,256]{2,1,0:T(8,128)(2,1)}, u32[]{:S(2)}) copy-start(bf16[2,8,256]{2,1,0:T(8,128)(2,1)} %param.14) | copy-start | bytes 24580
  39.1 66.4 %copy-start.1 = (f32[1,3,2,8,256]{4,3,2,1,0:T(8,128)S(1)}, f32[1,3,2,8,256]{4,3,2,1,0:T(8,128)}, u32[]{:S(2)}) copy-start(f32[1,3,2,8,256]{4,3,2,1,0:T(8,128)} %param.15) | copy-start | bytes 147460
  96.5 4.7 %collective-permute-start.1 = (f32[1,8,256]{2,1,0:T(8,128)S(1)}, f32[1,8,256]{2,1,0:T(8,128)S(1)}, u32[]{:S(2)}, u32[]{:S(2)}) collective-permute-start(f32[1,8,256]{2,1,0:T(8,128)S(1)} %get-tuple-element.7), channel_id=1, source_target_pairs={{0,4},{4,8},{8,12},{12,16},{16,20},{20,24},{24,28},{1,5},{5,9},{9,... | collective-permute-start | bytes 24584 | tf_op jit(solution)/shard_map/ppermute | solution.py:23
  99.9 5.5 %collective-permute-start = (f32[1,8,256]{2,1,0:T(8,128)S(1)}, f32[1,8,256]{2,1,0:T(8,128)S(1)}, u32[]{:S(2)}, u32[]{:S(2)}) collective-permute-start(f32[1,8,256]{2,1,0:T(8,128)S(1)} %get-tuple-element.6), channel_id=1, source_target_pairs={{4,0},{8,4},{12,8},{16,12},{20,16},{24,20},{28,24},{5,1},{9,5},{13... | collective-permute-start | bytes 24584 | tf_op jit(solution)/shard_map/ppermute | solution.py:25
  105.6 5.0 %collective-permute-start.3 = (f32[1,3,2,8,256]{4,3,2,1,0:T(8,128)S(1)}, f32[1,3,2,8,256]{4,3,2,1,0:T(8,128)S(1)}, u32[]{:S(2)}, u32[]{:S(2)}) collective-permute-start(f32[1,3,2,8,256]{4,3,2,1,0:T(8,128)S(1)} %maximum_add_fusion), channel_id=1, source_target_pairs={{1,0},{2,1},{3,2},{5,4},{6,5},{7,6},{9,8},{10,9},{11,10},{13,12},{... | collective-permute-start | bytes 147464 | tf_op jit(solution)/shard_map/ppermute | solution.py:25
  106.9 3.9 %collective-permute-start.2 = (f32[1,3,2,8,256]{4,3,2,1,0:T(8,128)S(1)}, f32[1,3,2,8,256]{4,3,2,1,0:T(8,128)S(1)}, u32[]{:S(2)}, u32[]{:S(2)}) collective-permute-start(f32[1,3,2,8,256]{4,3,2,1,0:T(8,128)S(1)} %maximum_add_fusion), channel_id=1, source_target_pairs={{0,1},{1,2},{2,3},{4,5},{5,6},{6,7},{8,9},{9,10},{10,11},{12,13},{... | collective-permute-start | bytes 147464 | tf_op jit(solution)/shard_map/ppermute | solution.py:23
where the time goes:
time: 113 us; the launch traced here: 111 us
  waiting for transfers between devices  54.2 us (48%)
  other arithmetic  23.6 us (21%)
  starting transfers between devices  19.9 us (18%)
  local copies, waits for them, and re-layouts  12.2 us (11%)
  between operations  1.51 us (1%)
    all_to_all x1, waiting for transfers between devices, shards(): lax.all_to_all(raw_data, 'space', split_axis=0, concat_axis=0, tiled=True)  45.7 us
    reduce_sum x1, other arithmetic, shards(): numerator = jnp.sum(weighted, axis=(0, 1))  11.1 us
    all_to_all x1, starting transfers between devices, shards(): lax.all_to_all(slot_info, 'space', split_axis=0, concat_axis=0, tiled=True)  7.31 us
    ppermute x2, starting transfers between devices, extended(): lax.ppermute(tail, axis, [(i, (i + 1) % count) for i in range(ends)])  6.41 us
    ppermute x2, waiting for transfers between devices, extended(): lax.ppermute(head, axis, [((i + 1) % count, i) for i in range(ends)])  4.2 us
    all_to_all x1, waiting for transfers between devices, shards(): lax.all_to_all(slot_info, 'space', split_axis=0, concat_axis=0, tiled=True)  4.09 us
    gather x2, other arithmetic, shards(): shift_slot = view_shift[view_of][tile_of].astype(jnp.bfloat16)  3.78 us
    gather x1, other arithmetic, shards(): frac_slot = view_frac[view_of][tile_of]  3.78 us
  transfers between devices with their start and end apart: 6, of which 4 were waited for; matrix products, arithmetic and copies ran while one was open for 3% of the time, Pallas kernels for 0%

commit v1 on v0

v1 whole, which is shorter than its diff:
```python
import functools

import jax
import jax.numpy as jnp
from jax import lax
from jax.experimental import pallas as pl
from jax.experimental.pallas import tpu as pltpu
from jax.sharding import PartitionSpec as P

KAPPA = 0.25
GROUP = 8


def join_kernel(bricks, shift_ref, frac_ref, tiles_ref, routes_ref, weights_ref, view_ref, out_ref):
    views = shift_ref.shape[0]
    top, tiles = routes_ref.shape
    rows = tiles_ref.shape[0] // tiles
    length = tiles_ref.shape[1]
    lanes = out_ref.shape[3]
    halves = length // lanes
    subs = out_ref.shape[2]
    layers = rows // subs
    group = min(GROUP, bricks)
    first = pl.program_id(0) * group
    single = bricks == group

    brick_ids = first + lax.broadcasted_iota(jnp.int32, (group, tiles), 0)
    by_brick = jnp.zeros((group, tiles), jnp.float32)
    for k in range(top):
        weight = weights_ref[k : k + 1, :].astype(jnp.float32)
        by_brick = by_brick + jnp.where(routes_ref[k : k + 1, :] == brick_ids, weight, 0.0)
    view_ids = lax.broadcasted_iota(jnp.int32, (8, tiles), 0)
    by_view = jnp.where(view_ref[...] == view_ids, 1.0, 0.0)

    width = tiles * rows
    spread = jnp.where(
        lax.broadcasted_iota(jnp.int32, (tiles, width), 1) // rows
        == lax.broadcasted_iota(jnp.int32, (tiles, width), 0),
        1.0,
        0.0,
    ).astype(jnp.bfloat16)
    both = jnp.concatenate([by_brick, by_view], axis=0).astype(jnp.bfloat16)
    wide = jnp.dot(both, spread, preferred_element_type=jnp.float32)
    wide_brick, wide_view = wide[:group], wide[group:]
    own_row = jnp.where(
        lax.broadcasted_iota(jnp.int32, (rows, width), 1) % rows
        == lax.broadcasted_iota(jnp.int32, (rows, width), 0),
        1.0,
        0.0,
    )

    lane = lax.broadcasted_iota(jnp.int32, (group * rows, length), 1)
    voxels = tiles_ref[...]
    total = jnp.zeros((group * rows, length), jnp.float32)
    for v in range(views):
        of_view = own_row * wide_view[v : v + 1]
        left = jnp.concatenate(
            [(of_view * wide_brick[b : b + 1]).astype(jnp.bfloat16) for b in range(group)], axis=0
        )
        summed = jnp.dot(left, voxels, preferred_element_type=jnp.float32)
        offset = shift_ref[v]
        fraction = frac_ref[v]
        here = pltpu.roll(summed, lax.rem(length - offset, length), 1)
        after = pltpu.roll(here, length - 1, 1)
        at = lane + offset
        total = total + jnp.where((at >= 0) & (at < length), (1.0 - fraction) * here, 0.0)
        total = total + jnp.where((at >= -1) & (at < length - 1), fraction * after, 0.0)

    tail = (layers + 2) * halves
    sums = jnp.broadcast_to(jnp.sum(by_brick, axis=1, keepdims=True), (group, lanes))

    def put(brick, slab, value):
        out_ref[brick, slab] = value

    def put_sum(brick, row, value):
        out_ref[brick, tail, row : row + 1, :] = value

    @pl.when(pl.program_id(0) == 0)
    def _():
        blank = jnp.zeros((subs, lanes), jnp.float32)
        for half in range(halves):
            put(0, half, blank)
            put(bricks - 1, (layers + 1) * halves + half, blank)
        if single:
            for b in range(bricks):
                put(b, tail, blank)
        else:
            out_ref[:, tail] = jnp.zeros((bricks, subs, lanes), jnp.float32)

    for b in range(group):
        brick = first + b if not single else b
        mine = [
            [
                total[b * rows + x * subs : b * rows + (x + 1) * subs, half * lanes : (half + 1) * lanes]
                for half in range(halves)
            ]
            for x in range(layers)
        ]
        for half in range(halves):
            for x in range(layers):
                put(brick, (1 + x) * halves + half, mine[x][half])
        put_sum(brick, 1, sums[b : b + 1])

        def before(brick=brick, b=b, mine=mine):
            for half in range(halves):
                put(brick - 1, (layers + 1) * halves + half, mine[0][half])
            put_sum(brick - 1, 2, sums[b : b + 1])

        def behind(brick=brick, b=b, mine=mine):
            for half in range(halves):
                put(brick + 1, half, mine[layers - 1][half])
            put_sum(brick + 1, 0, sums[b : b + 1])

        if b > 0:
            before()
        elif not single:
            pl.when(brick > 0)(before)
        if b < group - 1:
            behind()
        elif not single:
            pl.when(brick < bricks - 1)(behind)


def partial_sums(bricks, tiles, routes, weights, view, shift, frac):
    count, layers, subs, length = tiles.shape
    lanes = 128
    halves = length // lanes
    group = min(GROUP, bricks)
    whole = lambda shape: pl.BlockSpec(shape, lambda i: (0,) * len(shape))
    scalar = pl.BlockSpec(memory_space=pltpu.SMEM)
    flat = tiles.reshape(count * layers * subs, length)
    shape = (bricks, (layers + 2) * halves + 1, subs, lanes)
    return pl.pallas_call(
        functools.partial(join_kernel, bricks),
        grid=(bricks // group,),
        in_specs=[
            scalar,
            scalar,
            whole(flat.shape),
            whole(routes.shape),
            whole(weights.shape),
            whole(view.shape),
        ],
        out_specs=whole(shape),
        out_shape=jax.ShapeDtypeStruct(shape, jnp.float32),
        name="join_tiles",
    )(shift, frac.astype(jnp.float32), flat, routes, weights, view)


def shards(
    view_tiles,
    tile_routes,
    blend_weights,
    tile_view,
    view_shift,
    view_frac,
    atlas_image,
    displacement,
):
    nspace = lax.axis_size("space")
    ntime = lax.axis_size("tm")
    layers, subs, length = view_tiles.shape[2:]
    lanes = 128
    halves = length // lanes
    parts = partial_sums(
        nspace,
        view_tiles[0],
        tile_routes[0].T,
        blend_weights[0].T,
        tile_view,
        view_shift,
        view_frac,
    )
    summed = jnp.sum(lax.all_to_all(parts, "space", 0, 0, tiled=True), axis=0)
    numerator = summed[:-1].reshape(layers + 2, halves, subs, lanes)
    numerator = numerator.transpose(0, 2, 1, 3).reshape(layers + 2, subs, length)
    weight = summed[-1, :3, 0]
    joined_all = jnp.concatenate(
        [
            numerator[:1] / (1.0 + weight[0]),
            numerator[1:-1] / (1.0 + weight[1]),
            numerator[-1:] / (1.0 + weight[2]),
        ],
        axis=0,
    )
    joined = joined_all[1:-1]
    mismatch = joined - atlas_image.astype(jnp.float32)
    grad_x = (joined_all[2:] - joined_all[:-2]) * 0.5
    padded = jnp.pad(joined, ((0, 0), (1, 1), (1, 1)))
    grad_y = (padded[:, 2:, 1:-1] - padded[:, :-2, 1:-1]) * 0.5
    grad_z = (padded[:, 1:-1, 2:] - padded[:, 1:-1, :-2]) * 0.5
    scaled = mismatch / (
        grad_x * grad_x + grad_y * grad_y + grad_z * grad_z + mismatch * mismatch + 1.0
    )
    forces = jnp.stack([grad_x * scaled, grad_y * scaled, grad_z * scaled])
    stepped = displacement[0] + forces
    before = lax.ppermute(stepped, "tm", [(i, i + 1) for i in range(ntime - 1)])
    after = lax.ppermute(stepped, "tm", [(i + 1, i) for i in range(ntime - 1)])
    updated = stepped + KAPPA * (before - 2.0 * stepped + after)
    return (joined[None], updated[None])


def solution(mesh):
    in_specs = (
        P("tm", "space", None, None, None),
        P("tm", "space", None),
        P("tm", "space", None),
        P("tm", "space"),
        P(),
        P(),
        P("space", None, None),
        P("tm", None, "space", None, None),
    )
    out_specs = (P("tm", "space", None, None), P("tm", None, "space", None, None))
    return jax.shard_map(shards, mesh=mesh, in_specs=in_specs, out_specs=out_specs, check_vma=False)
```

time: 113 us -> 33.9 us (0.30)
  the two profiles are of different devices: /device:TPU:0 before, /device:TPU:1 now
where the time goes in v1:
time: 33.9 us; the launch traced here: 33.5 us
  blocking collectives  14.9 us (44%)
  starting transfers between devices  7.67 us (23%)
  Pallas kernels  2.64 us (8%)
  other arithmetic  2.62 us (8%)
  between operations  2.54 us (7%)
  local copies, waits for them, and re-layouts  1.93 us (6%)
  waiting for transfers between devices  1.15 us (3%)
    all_to_all x1, blocking collectives, shards(): summed = jnp.sum(lax.all_to_all(parts, 'space', 0, 0, tiled=True), axis=0)  14.9 us
    ppermute x1, starting transfers between devices, shards(): after = lax.ppermute(stepped, 'tm', [(i + 1, i) for i in range(ntime - 1)])  4.65 us
    ppermute x1, starting transfers between devices, shards(): before = lax.ppermute(stepped, 'tm', [(i, i + 1) for i in range(ntime - 1)])  3.02 us
    pallas_call x1, Pallas kernels, partial_sums(): pl.pallas_call(functools.partial(join_kernel, bricks), grid=(bricks // gr...  2.64 us
    unnamed x4, local copies, waits for them, and re-layouts  1.4 us
    convert_element_type x1, other arithmetic, partial_sums(): frac.astype(jnp.float32)  1.17 us
    ppermute x1, waiting for transfers between devices, shards(): before = lax.ppermute(stepped, 'tm', [(i, i + 1) for i in range(ntime - 1)])  1.15 us
  transfers between devices with their start and end apart: 2, of which 1 were waited for; matrix products, arithmetic and copies ran while one was open for 0% of the time, Pallas kernels for 0%

profile of v1, /device:TPU:1, one launch (start us, length us, event | category | flops | bytes accessed | tf_op | source)
XLA Modules:
  0.0 33.5 jit_solution(11525949198190492672)
XLA Ops:
  0.6 1.2 %convert_element_type.8.frac_ref = f32[5]{0:T(128)} convert(bf16[5]{0:T(256)(128)(2,1)} %param.13) | non-fusion elementwise | flops 5 | bytes 30 | tf_op jit(solution)/shard_map/convert_element_type | solution.py:147
  1.8 2.6 %join_tiles.1 = f32[8,9,8,128]{3,2,1,0:T(8,128)} custom-call(s32[5]{0:T(128)} %shift_ref.1, f32[5]{0:T(128)} %convert_element_type.8.frac_ref, bf16[1024,256]{1,0:T(8,128)(2,1)} %bitcast.33, s32[2,64]{1,0:T(2,128)} %bitcast.36, bf16[2,64]{1,0:T(2,128)(2,1)} %bitcast.37, s32[1,64]{1,0:T(1,128)} %view_ref.1), custom_call_target="tpu_custom_call" | custom-call | tf_op jit(solution)/shard_map/join_tiles/pallas_call | solution.py:133
  4.4 14.9 %all_to_all.5 = f32[8,9,8,128]{3,2,1,0:T(8,128)S(1)} all-to-all(f32[8,9,8,128]{3,2,1,0:T(8,128)} %join_tiles.1), channel_id=1, replica_groups=mesh['space'=8,'tm'=4] {'space'}, dimensions={0} | all-to-all | bytes 589824 | tf_op jit(solution)/shard_map/all_to_all | solution.py:174
  19.4 0.5 %fusion.10 = (f32[1,1,1]{2,1,0:T(1,128)}, f32[1,1,1]{2,1,0:T(1,128)}, f32[1,1,1]{2,1,0:T(1,128)}) fusion(f32[9,8,128]{2,1,0:T(8,128)S(1)} %reduce_sum.9), kind=kLoop, calls=%fused_computation.25 | loop fusion | bytes 24 | tf_op jit(solution)/shard_map/slice | solution.py:182
  21.8 0.6 %fusion.8 = (f32[2,8,256]{2,1,0:T(8,128)S(1)}, f32[1,2,8,256]{3,2,1,0:T(8,128)}) fusion(f32[]{:T(128)} %bitcast.7, f32[4,8,2,128]{3,1,2,0:T(8,128)S(1)} %bitcast.34), kind=kLoop, calls=%fused_computation.23 | loop fusion | flops 4096 | bytes 49156 | tf_op jit(solution)/shard_map/div | solution.py:181
  22.4 0.0 copy-start.1
  22.4 0.7 %copy-done.1 = bf16[2,8,256]{2,1,0:T(8,128)(2,1)S(1)} copy-done((bf16[2,8,256]{2,1,0:T(8,128)(2,1)S(1)}, bf16[2,8,256]{2,1,0:T(8,128)(2,1)}, u32[]{:S(2)}) %copy-start.1) | copy-done | bytes 8216
  23.1 0.1 multiply_bitcast_fusion.2
  23.2 0.0 copy-start
  23.2 0.1 multiply_bitcast_fusion.1
  23.3 0.7 %copy-done = f32[1,3,2,8,256]{4,3,2,1,0:T(8,128)S(1)} copy-done((f32[1,3,2,8,256]{4,3,2,1,0:T(8,128)S(1)}, f32[1,3,2,8,256]{4,3,2,1,0:T(8,128)}, u32[]{:S(2)}) %copy-start) | copy-done | bytes 49176
  24.0 4.6 %collective-permute-start.1 = (f32[3,2,8,256]{3,2,1,0:T(8,128)S(1)}, f32[3,2,8,256]{3,2,1,0:T(8,128)S(1)}, u32[]{:S(2)}, u32[]{:S(2)}) collective-permute-start(f32[3,2,8,256]{3,2,1,0:T(8,128)S(1)} %maximum_add_fusion), channel_id=1, source_target_pairs={{1,0},{2,1},{3,2},{5,4},{6,5},{7,6},{9,8},{10,9},{11,10},{13,12},{... | collective-permute-start | bytes 147464 | tf_op jit(solution)/shard_map/ppermute | solution.py:198
  28.6 3.0 %collective-permute-start = (f32[3,2,8,256]{3,2,1,0:T(8,128)S(1)}, f32[3,2,8,256]{3,2,1,0:T(8,128)S(1)}, u32[]{:S(2)}, u32[]{:S(2)}) collective-permute-start(f32[3,2,8,256]{3,2,1,0:T(8,128)S(1)} %maximum_add_fusion), channel_id=1, source_target_pairs={{0,1},{1,2},{2,3},{4,5},{5,6},{6,7},{8,9},{9,10},{10,11},{12,13},{... | collective-permute-start | bytes 147464 | tf_op jit(solution)/shard_map/ppermute | solution.py:197
  31.7 0.0 collective-permute-done.1
  31.7 1.1 %collective-permute-done = f32[3,2,8,256]{3,2,1,0:T(8,128)S(1)} collective-permute-done((f32[3,2,8,256]{3,2,1,0:T(8,128)S(1)}, f32[3,2,8,256]{3,2,1,0:T(8,128)S(1)}, u32[]{:S(2)}, u32[]{:S(2)}) %collective-permute-start) | collective-permute-done | bytes 49184 | tf_op jit(solution)/shard_map/ppermute | solution.py:197
  32.8 0.6 %add_bitcast_fusion = f32[1,3,2,8,256]{4,3,2,1,0:T(8,128)} fusion(f32[3,2,8,256]{3,2,1,0:T(8,128)S(1)} %collective-permute-done.1, f32[3,2,8,256]{3,2,1,0:T(8,128)S(1)} %collective-permute-done, f32[1,2,8,256]{3,2,1,0:T(8,128)S(1)} %get-tuple-element.8, f32[1,2,8,256]{3,2,1,0:T(8,128)S(1)} %get-tuple-element.7, f32[1,2,8,256]{3,2,1,0:T(8,128)S(1)} %get-tuple-element.2, ...), kind=kLoop, calls=%fused_computation.5 | loop fusion | flops 98304 | bytes 245760 | tf_op jit(solution)/shard_map/broadcast_in_dim | solution.py:200
  (4 shorter events, 0.0 us)
Async XLA Ops:
  22.4 0.7 %copy-start.1 = (bf16[2,8,256]{2,1,0:T(8,128)(2,1)S(1)}, bf16[2,8,256]{2,1,0:T(8,128)(2,1)}, u32[]{:S(2)}) copy-start(bf16[2,8,256]{2,1,0:T(8,128)(2,1)} %param.14) | copy-start | bytes 24580
  23.2 0.8 %copy-start = (f32[1,3,2,8,256]{4,3,2,1,0:T(8,128)S(1)}, f32[1,3,2,8,256]{4,3,2,1,0:T(8,128)}, u32[]{:S(2)}) copy-start(f32[1,3,2,8,256]{4,3,2,1,0:T(8,128)} %param.15) | copy-start | bytes 147460
  24.0 7.7 %collective-permute-start.1 = (f32[3,2,8,256]{3,2,1,0:T(8,128)S(1)}, f32[3,2,8,256]{3,2,1,0:T(8,128)S(1)}, u32[]{:S(2)}, u32[]{:S(2)}) collective-permute-start(f32[3,2,8,256]{3,2,1,0:T(8,128)S(1)} %maximum_add_fusion), channel_id=1, source_target_pairs={{1,0},{2,1},{3,2},{5,4},{6,5},{7,6},{9,8},{10,9},{11,10},{13,12},{... | collective-permute-start | bytes 147464 | tf_op jit(solution)/shard_map/ppermute | solution.py:198
  28.6 4.2 %collective-permute-start = (f32[3,2,8,256]{3,2,1,0:T(8,128)S(1)}, f32[3,2,8,256]{3,2,1,0:T(8,128)S(1)}, u32[]{:S(2)}, u32[]{:S(2)}) collective-permute-start(f32[3,2,8,256]{3,2,1,0:T(8,128)S(1)} %maximum_add_fusion), channel_id=1, source_target_pairs={{0,1},{1,2},{2,3},{4,5},{5,6},{6,7},{8,9},{9,10},{10,11},{12,13},{... | collective-permute-start | bytes 147464 | tf_op jit(solution)/shard_map/ppermute | solution.py:197

commit v2 on v1

--- a/solution.py
+++ b/solution.py
@@ -1,4 +1,5 @@
 import functools
+import math
 
 import jax
 import jax.numpy as jnp
@@ -8,10 +9,26 @@
 from jax.sharding import PartitionSpec as P
 
 KAPPA = 0.25
+VMEM_SPEC = pl.BlockSpec(memory_space=pltpu.VMEM)
+LANES = 128
+HELD_BYTES = 1 << 20
 GROUP = 8
 
 
-def join_kernel(bricks, shift_ref, frac_ref, tiles_ref, routes_ref, weights_ref, view_ref, out_ref):
+def join_kernel(
+    bricks,
+    shift_ref,
+    frac_ref,
+    tiles_ref,
+    routes_ref,
+    weights_ref,
+    view_ref,
+    atlas_ref,
+    field_ref,
+    out_ref,
+    atlas_out,
+    field_out,
+):
     views = shift_ref.shape[0]
     top, tiles = routes_ref.shape
     rows = tiles_ref.shape[0] // tiles
@@ -50,6 +67,7 @@
     )
 
     lane = lax.broadcasted_iota(jnp.int32, (group * rows, length), 1)
+    frac = frac_ref[...].astype(jnp.float32)
     voxels = tiles_ref[...]
     total = jnp.zeros((group * rows, length), jnp.float32)
     for v in range(views):
@@ -59,7 +77,7 @@
         )
         summed = jnp.dot(left, voxels, preferred_element_type=jnp.float32)
         offset = shift_ref[v]
-        fraction = frac_ref[v]
+        fraction = frac[:, v : v + 1]
         here = pltpu.roll(summed, lax.rem(length - offset, length), 1)
         after = pltpu.roll(here, length - 1, 1)
         at = lane + offset
@@ -77,6 +95,8 @@
 
     @pl.when(pl.program_id(0) == 0)
     def _():
+        atlas_out[...] = atlas_ref[...].astype(jnp.float32)
+        field_out[...] = field_ref[...]
         blank = jnp.zeros((subs, lanes), jnp.float32)
         for half in range(halves):
             put(0, half, blank)
@@ -121,30 +141,112 @@
             pl.when(brick < bricks - 1)(behind)
 
 
-def partial_sums(bricks, tiles, routes, weights, view, shift, frac):
+def held(x):
+    if x.size * x.dtype.itemsize > HELD_BYTES:
+        return x
+    return pltpu.with_memory_space_constraint(x, pltpu.VMEM)
+
+
+def output(shape):
+    if math.prod(shape) * 4 > HELD_BYTES:
+        return jax.ShapeDtypeStruct(shape, jnp.float32)
+    return pltpu.VMEM(shape, jnp.float32)
+
+
+def partial_sums(bricks, tiles, routes, weights, view, shift, frac, atlas, field):
     count, layers, subs, length = tiles.shape
-    lanes = 128
-    halves = length // lanes
+    halves = length // LANES
     group = min(GROUP, bricks)
     whole = lambda shape: pl.BlockSpec(shape, lambda i: (0,) * len(shape))
     scalar = pl.BlockSpec(memory_space=pltpu.SMEM)
     flat = tiles.reshape(count * layers * subs, length)
-    shape = (bricks, (layers + 2) * halves + 1, subs, lanes)
+    inputs = (flat, routes, weights, view, atlas, field)
+    frac = frac.reshape(1, -1)
     return pl.pallas_call(
         functools.partial(join_kernel, bricks),
         grid=(bricks // group,),
-        in_specs=[
-            scalar,
-            scalar,
-            whole(flat.shape),
-            whole(routes.shape),
-            whole(weights.shape),
-            whole(view.shape),
+        in_specs=[scalar, whole(frac.shape)] + [whole(each.shape) for each in inputs],
+        out_specs=[VMEM_SPEC, VMEM_SPEC, VMEM_SPEC],
+        out_shape=[
+            output((bricks, (layers + 2) * halves + 1, subs, LANES)),
+            output(atlas.shape),
+            output(field.shape),
         ],
-        out_specs=whole(shape),
-        out_shape=jax.ShapeDtypeStruct(shape, jnp.float32),
         name="join_tiles",
-    )(shift, frac.astype(jnp.float32), flat, routes, weights, view)
+    )(shift, frac, *inputs)
+
+
+def force_kernel(parts_ref, atlas_ref, field_ref, joined_ref, stepped_ref):
+    sources, slabs, subs, lanes = parts_ref.shape
+    layers, _, length = joined_ref.shape
+    halves = length // lanes
+
+    def total(slab):
+        value = parts_ref[0, slab]
+        for source in range(1, sources):
+            value = value + parts_ref[source, slab]
+        return value
+
+    sums = 1.0 + total(slabs - 1)
+    image = []
+    for x in range(layers + 2):
+        row = min(x, 1) + (x > layers)
+        below = jnp.broadcast_to(sums[row : row + 1], (subs, lanes))
+        image.append(
+            jnp.concatenate([total(x * halves + half) / below for half in range(halves)], axis=1)
+        )
+    sub = lax.broadcasted_iota(jnp.int32, (subs, length), 0)
+    lane = lax.broadcasted_iota(jnp.int32, (subs, length), 1)
+    for x in range(layers):
+        here = image[x + 1]
+        grad_x = (image[x + 2] - image[x]) * 0.5
+        up = jnp.where(sub == subs - 1, 0.0, pltpu.roll(here, subs - 1, 0))
+        down = jnp.where(sub == 0, 0.0, pltpu.roll(here, 1, 0))
+        grad_y = (up - down) * 0.5
+        right = jnp.where(lane == length - 1, 0.0, pltpu.roll(here, length - 1, 1))
+        left = jnp.where(lane == 0, 0.0, pltpu.roll(here, 1, 1))
+        grad_z = (right - left) * 0.5
+        mismatch = here - atlas_ref[x]
+        scaled = mismatch / (
+            grad_x * grad_x + grad_y * grad_y + grad_z * grad_z + mismatch * mismatch + 1.0
+        )
+        joined_ref[x] = here
+        stepped_ref[0, x] = field_ref[0, x] + grad_x * scaled
+        stepped_ref[1, x] = field_ref[1, x] + grad_y * scaled
+        stepped_ref[2, x] = field_ref[2, x] + grad_z * scaled
+
+
+def forces(parts, atlas, field):
+    return pl.pallas_call(
+        force_kernel,
+        in_specs=[VMEM_SPEC, VMEM_SPEC, VMEM_SPEC],
+        out_specs=[VMEM_SPEC, VMEM_SPEC],
+        out_shape=[output(atlas.shape), output(field.shape)],
+        name="forces",
+    )(held(parts), held(atlas), held(field))
+
+
+def smooth_kernel(stepped_ref, before_ref, after_ref, out_ref):
+    at = lax.axis_index("tm")
+    last = lax.axis_size("tm") - 1
+    middle = stepped_ref[...]
+    before = jnp.where(at > 0, before_ref[...], 0.0)
+    after = jnp.where(at < last, after_ref[...], 0.0)
+    out_ref[...] = middle + KAPPA * (before - 2.0 * middle + after)
+
+
+def smoothed(stepped):
+    count = lax.axis_size("tm")
+    forward = [(i, (i + 1) % count) for i in range(count)]
+    before = lax.ppermute(stepped, "tm", forward)
+    after = lax.ppermute(stepped, "tm", [(b, a) for a, b in forward])
+    return pl.pallas_call(
+        smooth_kernel,
+        in_specs=[VMEM_SPEC, VMEM_SPEC, VMEM_SPEC],
+        out_specs=VMEM_SPEC,
+        out_shape=jax.ShapeDtypeStruct(stepped.shape, jnp.float32),
+        name="smooth",
+    )(held(stepped), held(before), held(after))
 
 
 def shards(
@@ -157,46 +259,20 @@
     atlas_image,
     displacement,
 ):
-    nspace = lax.axis_size("space")
-    ntime = lax.axis_size("tm")
-    layers, subs, length = view_tiles.shape[2:]
-    lanes = 128
-    halves = length // lanes
-    parts = partial_sums(
-        nspace,
+    parts, atlas, field = partial_sums(
+        lax.axis_size("space"),
         view_tiles[0],
         tile_routes[0].T,
         blend_weights[0].T,
         tile_view,
         view_shift,
         view_frac,
+        atlas_image,
+        displacement[0],
     )
-    summed = jnp.sum(lax.all_to_all(parts, "space", 0, 0, tiled=True), axis=0)
-    numerator = summed[:-1].reshape(layers + 2, halves, subs, lanes)
-    numerator = numerator.transpose(0, 2, 1, 3).reshape(layers + 2, subs, length)
-    weight = summed[-1, :3, 0]
-    joined_all = jnp.concatenate(
-        [
-            numerator[:1] / (1.0 + weight[0]),
-            numerator[1:-1] / (1.0 + weight[1]),
-            numerator[-1:] / (1.0 + weight[2]),
-        ],
-        axis=0,
-    )
-    joined = joined_all[1:-1]
-    mismatch = joined - atlas_image.astype(jnp.float32)
-    grad_x = (joined_all[2:] - joined_all[:-2]) * 0.5
-    padded = jnp.pad(joined, ((0, 0), (1, 1), (1, 1)))
-    grad_y = (padded[:, 2:, 1:-1] - padded[:, :-2, 1:-1]) * 0.5
-    grad_z = (padded[:, 1:-1, 2:] - padded[:, 1:-1, :-2]) * 0.5
-    scaled = mismatch / (
-        grad_x * grad_x + grad_y * grad_y + grad_z * grad_z + mismatch * mismatch + 1.0
-    )
-    forces = jnp.stack([grad_x * scaled, grad_y * scaled, grad_z * scaled])
-    stepped = displacement[0] + forces
-    before = lax.ppermute(stepped, "tm", [(i, i + 1) for i in range(ntime - 1)])
-    after = lax.ppermute(stepped, "tm", [(i + 1, i) for i in range(ntime - 1)])
-    updated = stepped + KAPPA * (before - 2.0 * stepped + after)
+    parts = lax.all_to_all(parts, "space", 0, 0, tiled=True)
+    joined, stepped = forces(parts, atlas, field)
+    updated = smoothed(stepped)
     return (joined[None], updated[None])
 
 

time: 33.9 us -> 25.1 us (0.74)
  the two profiles are of different devices: /device:TPU:1 before, /device:TPU:0 now
where the time goes in v2:
time: 25.1 us; the launch traced here: 24.9 us
  blocking collectives  17.4 us (69%)
  waiting for transfers between devices  2.97 us (12%)
  Pallas kernels  2.66 us (11%)
  between operations  0.66 us (3%)
  local copies, waits for them, and re-layouts  0.6 us (2%)
  starting transfers between devices  0.55 us (2%)
    all_to_all x1, blocking collectives, shards(): parts = lax.all_to_all(parts, 'space', 0, 0, tiled=True)  17.4 us
    ppermute x1, waiting for transfers between devices, smoothed(): before = lax.ppermute(stepped, 'tm', forward)  2.33 us
    pallas_call x1, Pallas kernels, partial_sums(): pl.pallas_call(functools.partial(join_kernel, bricks), grid=(bricks // gr...  1.92 us
    ppermute x1, waiting for transfers between devices, smoothed(): after = lax.ppermute(stepped, 'tm', [(b, a) for a, b in forward])  0.64 us
    pallas_call x1, Pallas kernels, smoothed(): pl.pallas_call(smooth_kernel, in_specs=[VMEM_SPEC, VMEM_SPEC, VMEM_SPEC],...  0.63 us
    unnamed x1, local copies, waits for them, and re-layouts  0.6 us
  transfers between devices with their start and end apart: 2, of which 2 were waited for; matrix products, arithmetic and copies ran while one was open for 2% of the time, Pallas kernels for 0%

profile of v2, /device:TPU:0, one launch (start us, length us, event | category | flops | bytes accessed | tf_op | source)
XLA Modules:
  0.0 24.9 jit_solution(5094929184104152182)
XLA Ops:
  0.6 1.9 %join_tiles.1 = (f32[8,9,8,128]{3,2,1,0:T(8,128)S(1)}, f32[2,8,256]{2,1,0:T(8,128)S(1)}, f32[3,2,8,256]{3,2,1,0:T(8,128)S(1)}) custom-call(s32[5]{0:T(128)} %shift_ref.1, bf16[1,5]{1,0:T(2,128)(2,1)} %bitcast.16, bf16[1024,256]{1,0:T(8,128)(2,1)} %bitcast.12, s32[2,64]{1,0:T(2,128)} %bitcast.15, bf16[2,64]{1,0:T(2,128)(2,1)} %bitcast.17, s32[1,64]{1,0:T(1,128)} %view_ref.1, ...), custom_call_target="tpu_custom_call" | custom-call | tf_op jit(solution)/shard_map/join_tiles/pallas_call | solution.py:165
  2.6 17.4 %all_to_all.5.parts_ref = f32[8,9,8,128]{3,2,1,0:T(8,128)S(1)} all-to-all(f32[8,9,8,128]{3,2,1,0:T(8,128)S(1)} %get-tuple-element.7), channel_id=1, replica_groups=mesh['space'=8,'tm'=4] {'space'}, dimensions={0} | all-to-all | bytes 589824 | tf_op jit(solution)/shard_map/all_to_all | solution.py:273
  20.0 0.1 forces.1
  20.1 0.1 collective-permute-start.1
  20.2 0.5 %collective-permute-start = (f32[3,2,8,256]{3,2,1,0:T(8,128)S(1)}, f32[3,2,8,256]{3,2,1,0:T(8,128)S(1)}, u32[]{:S(2)}, u32[]{:S(2)}) collective-permute-start(f32[3,2,8,256]{3,2,1,0:T(8,128)S(1)} %get-tuple-element.11.stepped_ref), channel_id=1, source_target_pairs={{0,1},{1,2},{2,3},{3,0},{4,5},{5,6},{6,7},{7,4},{8,9},{9,10},{10,1... | collective-permute-start | bytes 147464 | tf_op jit(solution)/shard_map/ppermute | solution.py:241
  20.7 0.6 %copy.10 = f32[1,2,8,256]{3,2,1,0:T(8,128)} copy(f32[1,2,8,256]{3,2,1,0:T(8,128)S(1)} %bitcast.11) | data formatting | bytes 32768
  21.3 0.6 %collective-permute-done.1.after_ref = f32[3,2,8,256]{3,2,1,0:T(8,128)S(1)} collective-permute-done((f32[3,2,8,256]{3,2,1,0:T(8,128)S(1)}, f32[3,2,8,256]{3,2,1,0:T(8,128)S(1)}, u32[]{:S(2)}, u32[]{:S(2)}) %collective-permute-start.1) | collective-permute-done | bytes 49184 | tf_op jit(solution)/shard_map/ppermute | solution.py:242
  21.9 2.3 %collective-permute-done.before_ref = f32[3,2,8,256]{3,2,1,0:T(8,128)S(1)} collective-permute-done((f32[3,2,8,256]{3,2,1,0:T(8,128)S(1)}, f32[3,2,8,256]{3,2,1,0:T(8,128)S(1)}, u32[]{:S(2)}, u32[]{:S(2)}) %collective-permute-start) | collective-permute-done | bytes 49184 | tf_op jit(solution)/shard_map/ppermute | solution.py:241
  24.3 0.6 %smooth.1 = f32[3,2,8,256]{3,2,1,0:T(8,128)} custom-call(f32[3,2,8,256]{3,2,1,0:T(8,128)S(1)} %get-tuple-element.11.stepped_ref, f32[3,2,8,256]{3,2,1,0:T(8,128)S(1)} %collective-permute-done.before_ref, f32[3,2,8,256]{3,2,1,0:T(8,128)S(1)} %collective-permute-done.1.after_ref), custom_call_target="tpu_custom_call" | custom-call | tf_op jit(solution)/shard_map/smooth/pallas_call | solution.py:243
Async XLA Ops:
  20.1 1.8 %collective-permute-start.1 = (f32[3,2,8,256]{3,2,1,0:T(8,128)S(1)}, f32[3,2,8,256]{3,2,1,0:T(8,128)S(1)}, u32[]{:S(2)}, u32[]{:S(2)}) collective-permute-start(f32[3,2,8,256]{3,2,1,0:T(8,128)S(1)} %get-tuple-element.11.stepped_ref), channel_id=1, source_target_pairs={{1,0},{2,1},{3,2},{0,3},{5,4},{6,5},{7,6},{4,7},{9,8},{10,9},{11,1... | collective-permute-start | bytes 147464 | tf_op jit(solution)/shard_map/ppermute | solution.py:242
  20.2 4.1 %collective-permute-start = (f32[3,2,8,256]{3,2,1,0:T(8,128)S(1)}, f32[3,2,8,256]{3,2,1,0:T(8,128)S(1)}, u32[]{:S(2)}, u32[]{:S(2)}) collective-permute-start(f32[3,2,8,256]{3,2,1,0:T(8,128)S(1)} %get-tuple-element.11.stepped_ref), channel_id=1, source_target_pairs={{0,1},{1,2},{2,3},{3,0},{4,5},{5,6},{6,7},{7,4},{8,9},{9,10},{10,1... | collective-permute-start | bytes 147464 | tf_op jit(solution)/shard_map/ppermute | solution.py:241

commit v3 on v2

--- a/solution.py
+++ b/solution.py
@@ -12,6 +12,9 @@
 VMEM_SPEC = pl.BlockSpec(memory_space=pltpu.VMEM)
 LANES = 128
 HELD_BYTES = 1 << 20
+BITS = 22.0
+TINY = 1e-30
+EMPTY = 128 << 8
 GROUP = 8
 
 
@@ -28,15 +31,13 @@
     out_ref,
     atlas_out,
     field_out,
+    notes_ref,
 ):
     views = shift_ref.shape[0]
     top, tiles = routes_ref.shape
-    rows = tiles_ref.shape[0] // tiles
-    length = tiles_ref.shape[1]
+    _, layers, subs, length = tiles_ref.shape
     lanes = out_ref.shape[3]
     halves = length // lanes
-    subs = out_ref.shape[2]
-    layers = rows // subs
     group = min(GROUP, bricks)
     first = pl.program_id(0) * group
     single = bricks == group
@@ -49,9 +50,9 @@
     view_ids = lax.broadcasted_iota(jnp.int32, (8, tiles), 0)
     by_view = jnp.where(view_ref[...] == view_ids, 1.0, 0.0)
 
-    width = tiles * rows
+    width = tiles * subs
     spread = jnp.where(
-        lax.broadcasted_iota(jnp.int32, (tiles, width), 1) // rows
+        lax.broadcasted_iota(jnp.int32, (tiles, width), 1) // subs
         == lax.broadcasted_iota(jnp.int32, (tiles, width), 0),
         1.0,
         0.0,
@@ -60,76 +61,131 @@
     wide = jnp.dot(both, spread, preferred_element_type=jnp.float32)
     wide_brick, wide_view = wide[:group], wide[group:]
     own_row = jnp.where(
-        lax.broadcasted_iota(jnp.int32, (rows, width), 1) % rows
-        == lax.broadcasted_iota(jnp.int32, (rows, width), 0),
+        lax.broadcasted_iota(jnp.int32, (subs, width), 1) % subs
+        == lax.broadcasted_iota(jnp.int32, (subs, width), 0),
         1.0,
         0.0,
     )
-
-    lane = lax.broadcasted_iota(jnp.int32, (group * rows, length), 1)
+    left_all = jnp.concatenate([own_row * wide_brick[b : b + 1] for b in range(group)], axis=0)
+
     frac = frac_ref[...].astype(jnp.float32)
-    voxels = tiles_ref[...]
-    total = jnp.zeros((group * rows, length), jnp.float32)
+    lane = lax.broadcasted_iota(jnp.int32, (subs, lanes), 1)
+    left = jnp.concatenate(
+        [(left_all * wide_view[v : v + 1]).astype(jnp.bfloat16) for v in range(views)], axis=0
+    )
+    turns = []
     for v in range(views):
-        of_view = own_row * wide_view[v : v + 1]
-        left = jnp.concatenate(
-            [(of_view * wide_brick[b : b + 1]).astype(jnp.bfloat16) for b in range(group)], axis=0
-        )
-        summed = jnp.dot(left, voxels, preferred_element_type=jnp.float32)
         offset = shift_ref[v]
         fraction = frac[:, v : v + 1]
-        here = pltpu.roll(summed, lax.rem(length - offset, length), 1)
-        after = pltpu.roll(here, length - 1, 1)
         at = lane + offset
-        total = total + jnp.where((at >= 0) & (at < length), (1.0 - fraction) * here, 0.0)
-        total = total + jnp.where((at >= -1) & (at < length - 1), fraction * after, 0.0)
-
-    tail = (layers + 2) * halves
-    sums = jnp.broadcast_to(jnp.sum(by_brick, axis=1, keepdims=True), (group, lanes))
-
-    def put(brick, slab, value):
-        out_ref[brick, slab] = value
-
-    def put_sum(brick, row, value):
-        out_ref[brick, tail, row : row + 1, :] = value
+        factors = []
+        for half in range(halves):
+            voxel = at + half * lanes
+            valid = jnp.where((voxel >= 0) & (voxel < length), 1.0, 0.0)
+            ahead = valid
+            if half == 0:
+                ahead = jnp.where(lane == 0, jnp.where(offset < 0, 1.0, 0.0), valid)
+            factors.append(((1.0 - fraction) * valid, fraction * ahead))
+        turns.append((lax.rem(lanes - offset, lanes), (at >= 0) & (at < lanes), at < 0, factors))
+    last = lane == lanes - 1
+    total = []
+    for x in range(layers):
+        summed = jnp.dot(
+            left, tiles_ref[:, x].reshape(width, length), preferred_element_type=jnp.float32
+        )
+        near = [[None] * halves for _ in range(group)]
+        far = [[None] * halves for _ in range(group)]
+        for v, (amount, inside, under, factors) in enumerate(turns):
+            rolled = [
+                pltpu.roll(
+                    summed[
+                        v * group * subs : (v + 1) * group * subs, half * lanes : (half + 1) * lanes
+                    ],
+                    amount,
+                    1,
+                )
+                for half in range(halves)
+            ]
+            for b in range(group):
+                pieces = [part[b * subs : (b + 1) * subs] for part in rolled]
+                for half in range(halves):
+                    other = pieces[(half + 1) % halves]
+                    if halves > 2:
+                        other = jnp.where(under, pieces[half - 1], other)
+                    turned = jnp.where(inside, pieces[half], other)
+                    for sums, factor in zip((near, far), factors[half]):
+                        value = factor * turned
+                        old = sums[b][half]
+                        sums[b][half] = value if old is None else old + value
+        pieces = []
+        for b in range(group):
+            ahead = [pltpu.roll(part, lanes - 1, 1) for part in far[b]]
+            pieces.append(
+                [
+                    near[b][half] + jnp.where(last, ahead[(half + 1) % halves], ahead[half])
+                    for half in range(halves)
+                ]
+            )
+        total.append(pieces)
+
+    low = (layers + 2) * halves
+    tail = low + layers + 2
+    sums = jnp.sum(by_brick, axis=1, keepdims=True)
 
     @pl.when(pl.program_id(0) == 0)
     def _():
         atlas_out[...] = atlas_ref[...].astype(jnp.float32)
         field_out[...] = field_ref[...]
-        blank = jnp.zeros((subs, lanes), jnp.float32)
+        notes_ref[...] = jnp.full(notes_ref.shape, EMPTY, jnp.int32)
+        blank = jnp.zeros((subs, lanes), jnp.int16)
         for half in range(halves):
-            put(0, half, blank)
-            put(bricks - 1, (layers + 1) * halves + half, blank)
-        if single:
-            for b in range(bricks):
-                put(b, tail, blank)
-        else:
-            out_ref[:, tail] = jnp.zeros((bricks, subs, lanes), jnp.float32)
+            out_ref[0, half] = blank
+            out_ref[bricks - 1, (layers + 1) * halves + half] = blank
+        blank = jnp.full((subs, lanes), -32768, jnp.int16)
+        out_ref[0, low] = blank
+        out_ref[bricks - 1, low + layers + 1] = blank
+
+    def put_note(brick, place, whole, rest):
+        notes_ref[brick, place : place + 1, :] = whole
+        notes_ref[brick, place + 3 : place + 4, :] = rest
 
     for b in range(group):
         brick = first + b if not single else b
-        mine = [
-            [
-                total[b * rows + x * subs : b * rows + (x + 1) * subs, half * lanes : (half + 1) * lanes]
-                for half in range(halves)
+        largest = functools.reduce(
+            jnp.maximum, [jnp.abs(total[x][b][half]) for x in range(layers) for half in range(halves)]
+        )
+        largest = jnp.max(jnp.max(largest, axis=0, keepdims=True), axis=1, keepdims=True)
+        power = jnp.floor(jnp.log2(jnp.maximum(largest, TINY))) + 1.0
+        scale = jnp.exp2(BITS - power)
+        high, lows = [], []
+        for x in range(layers):
+            codes = [
+                jnp.round(total[x][b][half] * scale).astype(jnp.int32) for half in range(halves)
             ]
-            for x in range(layers)
-        ]
-        for half in range(halves):
-            for x in range(layers):
-                put(brick, (1 + x) * halves + half, mine[x][half])
-        put_sum(brick, 1, sums[b : b + 1])
-
-        def before(brick=brick, b=b, mine=mine):
+            high.append([(code >> 8).astype(jnp.int16) for code in codes])
+            lows.append((((codes[1] & 255) << 8) + (codes[0] & 255) - 32768).astype(jnp.int16))
+        weight = sums[b : b + 1] * 256.0
+        weight = jnp.broadcast_to(weight, (1, lanes)).astype(jnp.int32)
+        power = jnp.broadcast_to(power, (1, lanes)).astype(jnp.int32)
+        note = (weight >> 8, (weight & 255) + ((power + 128) << 8))
+
+        for x in range(layers):
             for half in range(halves):
-                put(brick - 1, (layers + 1) * halves + half, mine[0][half])
-            put_sum(brick - 1, 2, sums[b : b + 1])
-
-        def behind(brick=brick, b=b, mine=mine):
+                out_ref[brick, (1 + x) * halves + half] = high[x][half]
+            out_ref[brick, low + 1 + x] = lows[x]
+        put_note(brick, 1, *note)
+
+        def before(brick=brick, high=high, lows=lows, note=note):
             for half in range(halves):
-                put(brick + 1, half, mine[layers - 1][half])
-            put_sum(brick + 1, 0, sums[b : b + 1])
+                out_ref[brick - 1, (layers + 1) * halves + half] = high[0][half]
+            out_ref[brick - 1, low + layers + 1] = lows[0]
+            put_note(brick - 1, 2, *note)
+
+        def behind(brick=brick, high=high, lows=lows, note=note):
+            for half in range(halves):
+                out_ref[brick + 1, half] = high[layers - 1][half]
+            out_ref[brick + 1, low] = lows[layers - 1]
+            put_note(brick + 1, 0, *note)
 
         if b > 0:
             before()
@@ -140,6 +196,11 @@
         elif not single:
             pl.when(brick < bricks - 1)(behind)
 
+    @pl.when(pl.program_id(0) == pl.num_programs(0) - 1)
+    def _():
+        for d in range(bricks):
+            out_ref[d, tail] = (notes_ref[d] - 32768).astype(jnp.int16)
+
 
 def held(x):
     if x.size * x.dtype.itemsize > HELD_BYTES:
@@ -147,20 +208,19 @@
     return pltpu.with_memory_space_constraint(x, pltpu.VMEM)
 
 
-def output(shape):
-    if math.prod(shape) * 4 > HELD_BYTES:
-        return jax.ShapeDtypeStruct(shape, jnp.float32)
-    return pltpu.VMEM(shape, jnp.float32)
+def output(shape, dtype=jnp.float32):
+    if math.prod(shape) * jnp.dtype(dtype).itemsize > HELD_BYTES:
+        return jax.ShapeDtypeStruct(shape, dtype)
+    return pltpu.VMEM(shape, dtype)
 
 
 def partial_sums(bricks, tiles, routes, weights, view, shift, frac, atlas, field):
-    count, layers, subs, length = tiles.shape
+    _, layers, subs, length = tiles.shape
     halves = length // LANES
     group = min(GROUP, bricks)
     whole = lambda shape: pl.BlockSpec(shape, lambda i: (0,) * len(shape))
     scalar = pl.BlockSpec(memory_space=pltpu.SMEM)
-    flat = tiles.reshape(count * layers * subs, length)
-    inputs = (flat, routes, weights, view, atlas, field)
+    inputs = (tiles, routes, weights, view, atlas, field)
     frac = frac.reshape(1, -1)
     return pl.pallas_call(
         functools.partial(join_kernel, bricks),
@@ -168,10 +228,11 @@
         in_specs=[scalar, whole(frac.shape)] + [whole(each.shape) for each in inputs],
         out_specs=[VMEM_SPEC, VMEM_SPEC, VMEM_SPEC],
         out_shape=[
-            output((bricks, (layers + 2) * halves + 1, subs, LANES)),
+            output((bricks, (layers + 2) * (halves + 1) + 1, subs, LANES), jnp.int16),
             output(atlas.shape),
             output(field.shape),
         ],
+        scratch_shapes=[pltpu.VMEM((bricks, subs, LANES), jnp.int32)],
         name="join_tiles",
     )(shift, frac, *inputs)
 
@@ -181,20 +242,28 @@
     layers, _, length = joined_ref.shape
     halves = length // lanes
 
-    def total(slab):
-        value = parts_ref[0, slab]
-        for source in range(1, sources):
-            value = value + parts_ref[source, slab]
-        return value
-
-    sums = 1.0 + total(slabs - 1)
+    low = (layers + 2) * halves
+    wholes, rests = 0, 0
+    numerator = [[0.0] * halves for _ in range(layers + 2)]
+    for source in range(sources):
+        note = parts_ref[source, slabs - 1].astype(jnp.int32) + 32768
+        wholes = wholes + note
+        rests = rests + (note & 255)
+        scale = jnp.exp2(((note >> 8) - 128).astype(jnp.float32) - BITS)
+        for x in range(layers + 2):
+            place = 3 + min(x, 1) + (x > layers)
+            factor = jnp.broadcast_to(scale[place : place + 1], (subs, lanes))
+            pair = parts_ref[source, low + x].astype(jnp.int32) + 32768
+            for half, byte in enumerate((pair & 255, pair >> 8)):
+                code = (parts_ref[source, x * halves + half].astype(jnp.int32) << 8) + byte
+                numerator[x][half] = numerator[x][half] + code.astype(jnp.float32) * factor
     image = []
     for x in range(layers + 2):
-        row = min(x, 1) + (x > layers)
-        below = jnp.broadcast_to(sums[row : row + 1], (subs, lanes))
-        image.append(
-            jnp.concatenate([total(x * halves + half) / below for half in range(halves)], axis=1)
-        )
+        place = min(x, 1) + (x > layers)
+        weight = wholes[place : place + 1].astype(jnp.float32)
+        weight = weight + rests[place + 3 : place + 4].astype(jnp.float32) * (1.0 / 256.0)
+        below = jnp.broadcast_to(1.0 + weight, (subs, lanes))
+        image.append(jnp.concatenate([part / below for part in numerator[x]], axis=1))
     sub = lax.broadcasted_iota(jnp.int32, (subs, length), 0)
     lane = lax.broadcasted_iota(jnp.int32, (subs, length), 1)
     for x in range(layers):

time: 25.1 us -> 22.9 us (0.912)
  blocking collectives: 17.4 us -> 15.3 us
    all_to_all x1, blocking collectives: 17.4 us -> 15.3 us  [shards(): parts = lax.all_to_all(parts, 'space', 0, 0, tiled=True)]
  transfers between devices with their start and end apart: 2 -> 2, of which waited for: 2 -> 2; matrix products, arithmetic and copies ran while one was open for 2% -> 3% of each run, Pallas kernels for 0% -> 0%
where the time goes in v3:
time: 22.9 us; the launch traced here: 22.7 us
  blocking collectives  15.3 us (67%)
  waiting for transfers between devices  2.97 us (13%)
  Pallas kernels  2.62 us (11%)
  between operations  0.66 us (3%)
  local copies, waits for them, and re-layouts  0.6 us (3%)
  starting transfers between devices  0.55 us (2%)
    all_to_all x1, blocking collectives, shards(): parts = lax.all_to_all(parts, 'space', 0, 0, tiled=True)  15.3 us
    ppermute x1, waiting for transfers between devices, smoothed(): before = lax.ppermute(stepped, 'tm', forward)  2.33 us
    pallas_call x1, Pallas kernels, partial_sums(): pl.pallas_call(functools.partial(join_kernel, bricks), grid=(bricks // gr...  1.85 us
    ppermute x1, waiting for transfers between devices, smoothed(): after = lax.ppermute(stepped, 'tm', [(b, a) for a, b in forward])  0.64 us
    pallas_call x1, Pallas kernels, smoothed(): pl.pallas_call(smooth_kernel, in_specs=[VMEM_SPEC, VMEM_SPEC, VMEM_SPEC],...  0.63 us
    unnamed x1, local copies, waits for them, and re-layouts  0.6 us
    ppermute x1, starting transfers between devices, smoothed(): before = lax.ppermute(stepped, 'tm', forward)  0.5 us
  transfers between devices with their start and end apart: 2, of which 2 were waited for; matrix products, arithmetic and copies ran while one was open for 3% of the time, Pallas kernels for 0%

profile of v3, /device:TPU:0, one launch (start us, length us, event | category | flops | bytes accessed | tf_op | source)
XLA Modules:
  0.0 22.7 jit_solution(17645890221931309627)
XLA Ops:
  0.6 1.9 %join_tiles.1 = (s16[8,13,8,128]{3,2,1,0:T(8,128)(2,1)S(1)}, f32[2,8,256]{2,1,0:T(8,128)S(1)}, f32[3,2,8,256]{3,2,1,0:T(8,128)S(1)}) custom-call(s32[5]{0:T(128)} %shift_ref.1, bf16[1,5]{1,0:T(2,128)(2,1)} %bitcast.16, bf16[64,2,8,256]{3,2,1,0:T(8,128)(2,1)} %bitcast.12, s32[2,64]{1,0:T(2,128)} %bitcast.15, bf16[2,64]{1,0:T(2,128)(2,1)} %bitcast.17, ...), custom_call_target="tpu_custom_call" | custom-call | tf_op jit(solution)/shard_map/join_tiles/pallas_call | solution.py:225
  2.5 15.3 %all_to_all.5.parts_ref = s16[8,13,8,128]{3,2,1,0:T(8,128)(2,1)S(1)} all-to-all(s16[8,13,8,128]{3,2,1,0:T(8,128)(2,1)S(1)} %get-tuple-element.7), channel_id=1, replica_groups=mesh['space'=8,'tm'=4] {'space'}, dimensions={0} | all-to-all | bytes 425984 | tf_op jit(solution)/shard_map/all_to_all | solution.py:342
  17.8 0.1 forces.1
  17.9 0.1 collective-permute-start.1
  18.0 0.5 %collective-permute-start = (f32[3,2,8,256]{3,2,1,0:T(8,128)S(1)}, f32[3,2,8,256]{3,2,1,0:T(8,128)S(1)}, u32[]{:S(2)}, u32[]{:S(2)}) collective-permute-start(f32[3,2,8,256]{3,2,1,0:T(8,128)S(1)} %get-tuple-element.11.stepped_ref), channel_id=1, source_target_pairs={{0,1},{1,2},{2,3},{3,0},{4,5},{5,6},{6,7},{7,4},{8,9},{9,10},{10,1... | collective-permute-start | bytes 147464 | tf_op jit(solution)/shard_map/ppermute | solution.py:310
  18.5 0.6 %copy.10 = f32[1,2,8,256]{3,2,1,0:T(8,128)} copy(f32[1,2,8,256]{3,2,1,0:T(8,128)S(1)} %bitcast.11) | data formatting | bytes 32768
  19.1 0.6 %collective-permute-done.1.after_ref = f32[3,2,8,256]{3,2,1,0:T(8,128)S(1)} collective-permute-done((f32[3,2,8,256]{3,2,1,0:T(8,128)S(1)}, f32[3,2,8,256]{3,2,1,0:T(8,128)S(1)}, u32[]{:S(2)}, u32[]{:S(2)}) %collective-permute-start.1) | collective-permute-done | bytes 49184 | tf_op jit(solution)/shard_map/ppermute | solution.py:311
  19.7 2.3 %collective-permute-done.before_ref = f32[3,2,8,256]{3,2,1,0:T(8,128)S(1)} collective-permute-done((f32[3,2,8,256]{3,2,1,0:T(8,128)S(1)}, f32[3,2,8,256]{3,2,1,0:T(8,128)S(1)}, u32[]{:S(2)}, u32[]{:S(2)}) %collective-permute-start) | collective-permute-done | bytes 49184 | tf_op jit(solution)/shard_map/ppermute | solution.py:310
  22.1 0.6 %smooth.1 = f32[3,2,8,256]{3,2,1,0:T(8,128)} custom-call(f32[3,2,8,256]{3,2,1,0:T(8,128)S(1)} %get-tuple-element.11.stepped_ref, f32[3,2,8,256]{3,2,1,0:T(8,128)S(1)} %collective-permute-done.before_ref, f32[3,2,8,256]{3,2,1,0:T(8,128)S(1)} %collective-permute-done.1.after_ref), custom_call_target="tpu_custom_call" | custom-call | tf_op jit(solution)/shard_map/smooth/pallas_call | solution.py:312
Async XLA Ops:
  17.9 1.8 %collective-permute-start.1 = (f32[3,2,8,256]{3,2,1,0:T(8,128)S(1)}, f32[3,2,8,256]{3,2,1,0:T(8,128)S(1)}, u32[]{:S(2)}, u32[]{:S(2)}) collective-permute-start(f32[3,2,8,256]{3,2,1,0:T(8,128)S(1)} %get-tuple-element.11.stepped_ref), channel_id=1, source_target_pairs={{1,0},{2,1},{3,2},{0,3},{5,4},{6,5},{7,6},{4,7},{9,8},{10,9},{11,1... | collective-permute-start | bytes 147464 | tf_op jit(solution)/shard_map/ppermute | solution.py:311
  18.0 4.1 %collective-permute-start = (f32[3,2,8,256]{3,2,1,0:T(8,128)S(1)}, f32[3,2,8,256]{3,2,1,0:T(8,128)S(1)}, u32[]{:S(2)}, u32[]{:S(2)}) collective-permute-start(f32[3,2,8,256]{3,2,1,0:T(8,128)S(1)} %get-tuple-element.11.stepped_ref), channel_id=1, source_target_pairs={{0,1},{1,2},{2,3},{3,0},{4,5},{5,6},{6,7},{7,4},{8,9},{9,10},{10,1... | collective-permute-start | bytes 147464 | tf_op jit(solution)/shard_map/ppermute | solution.py:310

commit v4 on v3

--- a/solution.py
+++ b/solution.py
@@ -12,8 +12,8 @@
 VMEM_SPEC = pl.BlockSpec(memory_space=pltpu.VMEM)
 LANES = 128
 HELD_BYTES = 1 << 20
-BITS = 22.0
 TINY = 1e-30
+LIMIT = 32767.0
 EMPTY = 128 << 8
 GROUP = 8
 
@@ -128,8 +128,7 @@
             )
         total.append(pieces)
 
-    low = (layers + 2) * halves
-    tail = low + layers + 2
+    tail = (layers + 2) * halves
     sums = jnp.sum(by_brick, axis=1, keepdims=True)
 
     @pl.when(pl.program_id(0) == 0)
@@ -141,9 +140,6 @@
         for half in range(halves):
             out_ref[0, half] = blank
             out_ref[bricks - 1, (layers + 1) * halves + half] = blank
-        blank = jnp.full((subs, lanes), -32768, jnp.int16)
-        out_ref[0, low] = blank
-        out_ref[bricks - 1, low + layers + 1] = blank
 
     def put_note(brick, place, whole, rest):
         notes_ref[brick, place : place + 1, :] = whole
@@ -151,19 +147,10 @@
 
     for b in range(group):
         brick = first + b if not single else b
-        largest = functools.reduce(
-            jnp.maximum, [jnp.abs(total[x][b][half]) for x in range(layers) for half in range(halves)]
+        power, scale = scale_of(
+            [total[x][b][half] for x in range(layers) for half in range(halves)]
         )
-        largest = jnp.max(jnp.max(largest, axis=0, keepdims=True), axis=1, keepdims=True)
-        power = jnp.floor(jnp.log2(jnp.maximum(largest, TINY))) + 1.0
-        scale = jnp.exp2(BITS - power)
-        high, lows = [], []
-        for x in range(layers):
-            codes = [
-                jnp.round(total[x][b][half] * scale).astype(jnp.int32) for half in range(halves)
-            ]
-            high.append([(code >> 8).astype(jnp.int16) for code in codes])
-            lows.append((((codes[1] & 255) << 8) + (codes[0] & 255) - 32768).astype(jnp.int16))
+        codes = [[coded(part, scale) for part in total[x][b]] for x in range(layers)]
         weight = sums[b : b + 1] * 256.0
         weight = jnp.broadcast_to(weight, (1, lanes)).astype(jnp.int32)
         power = jnp.broadcast_to(power, (1, lanes)).astype(jnp.int32)
@@ -171,20 +158,17 @@
 
         for x in range(layers):
             for half in range(halves):
-                out_ref[brick, (1 + x) * halves + half] = high[x][half]
-            out_ref[brick, low + 1 + x] = lows[x]
+                out_ref[brick, (1 + x) * halves + half] = codes[x][half]
         put_note(brick, 1, *note)
 
-        def before(brick=brick, high=high, lows=lows, note=note):
-            for half in range(halves):
-                out_ref[brick - 1, (layers + 1) * halves + half] = high[0][half]
-            out_ref[brick - 1, low + layers + 1] = lows[0]
+        def before(brick=brick, codes=codes, note=note):
+            for half in range(halves):
+                out_ref[brick - 1, (layers + 1) * halves + half] = codes[0][half]
             put_note(brick - 1, 2, *note)
 
-        def behind(brick=brick, high=high, lows=lows, note=note):
-            for half in range(halves):
-                out_ref[brick + 1, half] = high[layers - 1][half]
-            out_ref[brick + 1, low] = lows[layers - 1]
+        def behind(brick=brick, codes=codes, note=note):
+            for half in range(halves):
+                out_ref[brick + 1, half] = codes[layers - 1][half]
             put_note(brick + 1, 0, *note)
 
         if b > 0:
@@ -228,7 +212,7 @@
         in_specs=[scalar, whole(frac.shape)] + [whole(each.shape) for each in inputs],
         out_specs=[VMEM_SPEC, VMEM_SPEC, VMEM_SPEC],
         out_shape=[
-            output((bricks, (layers + 2) * (halves + 1) + 1, subs, LANES), jnp.int16),
+            output((bricks, (layers + 2) * halves + 1, subs, LANES), jnp.int16),
             output(atlas.shape),
             output(field.shape),
         ],
@@ -237,25 +221,34 @@
     )(shift, frac, *inputs)
 
 
-def force_kernel(parts_ref, atlas_ref, field_ref, joined_ref, stepped_ref):
+def scale_of(parts):
+    largest = functools.reduce(jnp.maximum, [jnp.abs(part) for part in parts])
+    largest = jnp.max(jnp.max(largest, axis=0, keepdims=True), axis=1, keepdims=True)
+    power = jnp.floor(jnp.log2(jnp.maximum(largest, TINY))) + 1.0
+    return power, jnp.exp2(15.0 - power)
+
+
+def coded(part, scale):
+    return jnp.clip(jnp.round(part * scale), -LIMIT, LIMIT).astype(jnp.int32).astype(jnp.int16)
+
+
+def force_kernel(parts_ref, atlas_ref, field_ref, joined_ref, stepped_ref, codes_ref):
     sources, slabs, subs, lanes = parts_ref.shape
     layers, _, length = joined_ref.shape
     halves = length // lanes
 
-    low = (layers + 2) * halves
     wholes, rests = 0, 0
     numerator = [[0.0] * halves for _ in range(layers + 2)]
     for source in range(sources):
         note = parts_ref[source, slabs - 1].astype(jnp.int32) + 32768
         wholes = wholes + note
         rests = rests + (note & 255)
-        scale = jnp.exp2(((note >> 8) - 128).astype(jnp.float32) - BITS)
+        scale = jnp.exp2(((note >> 8) - 128).astype(jnp.float32) - 15.0)
         for x in range(layers + 2):
             place = 3 + min(x, 1) + (x > layers)
             factor = jnp.broadcast_to(scale[place : place + 1], (subs, lanes))
-            pair = parts_ref[source, low + x].astype(jnp.int32) + 32768
-            for half, byte in enumerate((pair & 255, pair >> 8)):
-                code = (parts_ref[source, x * halves + half].astype(jnp.int32) << 8) + byte
+            for half in range(halves):
+                code = parts_ref[source, x * halves + half].astype(jnp.int32)
                 numerator[x][half] = numerator[x][half] + code.astype(jnp.float32) * factor
     image = []
     for x in range(layers + 2):
@@ -266,6 +259,7 @@
         image.append(jnp.concatenate([part / below for part in numerator[x]], axis=1))
     sub = lax.broadcasted_iota(jnp.int32, (subs, length), 0)
     lane = lax.broadcasted_iota(jnp.int32, (subs, length), 1)
+    stepped = []
     for x in range(layers):
         here = image[x + 1]
         grad_x = (image[x + 2] - image[x]) * 0.5
@@ -280,17 +274,29 @@
             grad_x * grad_x + grad_y * grad_y + grad_z * grad_z + mismatch * mismatch + 1.0
         )
         joined_ref[x] = here
-        stepped_ref[0, x] = field_ref[0, x] + grad_x * scaled
-        stepped_ref[1, x] = field_ref[1, x] + grad_y * scaled
-        stepped_ref[2, x] = field_ref[2, x] + grad_z * scaled
+        for c, grad in enumerate((grad_x, grad_y, grad_z)):
+            value = field_ref[c, x] + grad * scaled
+            stepped_ref[c, x] = value
+            for half in range(halves):
+                part = value[:, half * lanes : (half + 1) * lanes]
+                stepped.append(((c * layers + x) * halves + half, part))
+    power, scale = scale_of([part for _, part in stepped])
+    for slab, part in stepped:
+        codes_ref[slab] = coded(part, scale)
+    codes_ref[len(stepped)] = jnp.broadcast_to(power, (subs, lanes)).astype(jnp.int32).astype(jnp.int16)
 
 
 def forces(parts, atlas, field):
+    subs = field.shape[2]
     return pl.pallas_call(
         force_kernel,
         in_specs=[VMEM_SPEC, VMEM_SPEC, VMEM_SPEC],
-        out_specs=[VMEM_SPEC, VMEM_SPEC],
-        out_shape=[output(atlas.shape), output(field.shape)],
+        out_specs=[VMEM_SPEC, VMEM_SPEC, VMEM_SPEC],
+        out_shape=[
+            output(atlas.shape),
+            output(field.shape),
+            output((field.size // (subs * LANES) + 1, subs, LANES), jnp.int16),
+        ],
         name="forces",
     )(held(parts), held(atlas), held(field))
 
@@ -298,17 +304,33 @@
 def smooth_kernel(stepped_ref, before_ref, after_ref, out_ref):
     at = lax.axis_index("tm")
     last = lax.axis_size("tm") - 1
-    middle = stepped_ref[...]
-    before = jnp.where(at > 0, before_ref[...], 0.0)
-    after = jnp.where(at < last, after_ref[...], 0.0)
-    out_ref[...] = middle + KAPPA * (before - 2.0 * middle + after)
-
-
-def smoothed(stepped):
+    fields, layers, _, length = stepped_ref.shape
+    slabs, _, lanes = before_ref.shape
+    halves = length // lanes
+    there = [
+        (ref, jnp.exp2(ref[slabs - 1].astype(jnp.int32).astype(jnp.float32) - 15.0), inner)
+        for ref, inner in ((before_ref, at > 0), (after_ref, at < last))
+    ]
+    for c in range(fields):
+        for x in range(layers):
+            others = []
+            for half in range(halves):
+                slab = (c * layers + x) * halves + half
+                values = [
+                    jnp.where(inner, ref[slab].astype(jnp.int32).astype(jnp.float32) * step, 0.0)
+                    for ref, step, inner in there
+                ]
+                others.append(values[0] + values[1])
+            middle = stepped_ref[c, x]
+            others = jnp.concatenate(others, axis=1)
+            out_ref[c, x] = middle + KAPPA * (others - 2.0 * middle)
+
+
+def smoothed(stepped, codes):
     count = lax.axis_size("tm")
     forward = [(i, (i + 1) % count) for i in range(count)]
-    before = lax.ppermute(stepped, "tm", forward)
-    after = lax.ppermute(stepped, "tm", [(b, a) for a, b in forward])
+    before = lax.ppermute(codes, "tm", forward)
+    after = lax.ppermute(codes, "tm", [(b, a) for a, b in forward])
     return pl.pallas_call(
         smooth_kernel,
         in_specs=[VMEM_SPEC, VMEM_SPEC, VMEM_SPEC],
@@ -340,8 +362,8 @@
         displacement[0],
     )
     parts = lax.all_to_all(parts, "space", 0, 0, tiled=True)
-    joined, stepped = forces(parts, atlas, field)
-    updated = smoothed(stepped)
+    joined, stepped, codes = forces(parts, atlas, field)
+    updated = smoothed(stepped, codes)
     return (joined[None], updated[None])
 
 

time: 22.9 us -> 21.8 us (0.952)
  blocking collectives: 15.3 us -> 14.6 us
  waiting for transfers between devices: 2.97 us -> 2.49 us
    all_to_all x1, blocking collectives: 15.3 us -> 14.6 us  [shards(): parts = lax.all_to_all(parts, 'space', 0, 0, tiled=True)]
    ppermute x2, waiting for transfers between devices: 2.97 us -> 2.49 us  [the longest x1 2.06 us: smoothed(): before = lax.ppermute(codes, 'tm', forward)]
where the time goes in v4:
time: 21.8 us; the launch traced here: 21.6 us
  blocking collectives  14.6 us (67%)
  Pallas kernels  2.72 us (12%)
  waiting for transfers between devices  2.49 us (11%)
  between operations  0.66 us (3%)
  local copies, waits for them, and re-layouts  0.6 us (3%)
  starting transfers between devices  0.55 us (3%)
    all_to_all x1, blocking collectives, shards(): parts = lax.all_to_all(parts, 'space', 0, 0, tiled=True)  14.6 us
    ppermute x1, waiting for transfers between devices, smoothed(): before = lax.ppermute(codes, 'tm', forward)  2.06 us
    pallas_call x1, Pallas kernels, partial_sums(): pl.pallas_call(functools.partial(join_kernel, bricks), grid=(bricks // gr...  1.84 us
    pallas_call x1, Pallas kernels, smoothed(): pl.pallas_call(smooth_kernel, in_specs=[VMEM_SPEC, VMEM_SPEC, VMEM_SPEC],...  0.65 us
    unnamed x1, local copies, waits for them, and re-layouts  0.6 us
    ppermute x1, starting transfers between devices, smoothed(): before = lax.ppermute(codes, 'tm', forward)  0.5 us
  transfers between devices with their start and end apart: 2, of which 2 were waited for; matrix products, arithmetic and copies ran while one was open for 3% of the time, Pallas kernels for 0%

profile of v4, /device:TPU:0, one launch (start us, length us, event | category | flops | bytes accessed | tf_op | source)
XLA Modules:
  0.0 21.6 jit_solution(7438697336224017173)
XLA Ops:
  0.6 1.8 %join_tiles.1 = (s16[8,9,8,128]{3,2,1,0:T(8,128)(2,1)S(1)}, f32[2,8,256]{2,1,0:T(8,128)S(1)}, f32[3,2,8,256]{3,2,1,0:T(8,128)S(1)}) custom-call(s32[5]{0:T(128)} %shift_ref.1, bf16[1,5]{1,0:T(2,128)(2,1)} %bitcast.16, bf16[64,2,8,256]{3,2,1,0:T(8,128)(2,1)} %bitcast.12, s32[2,64]{1,0:T(2,128)} %bitcast.15, bf16[2,64]{1,0:T(2,128)(2,1)} %bitcast.17, ...), custom_call_target="tpu_custom_call" | custom-call | tf_op jit(solution)/shard_map/join_tiles/pallas_call | solution.py:209
  2.5 14.6 %all_to_all.5.parts_ref = s16[8,9,8,128]{3,2,1,0:T(8,128)(2,1)S(1)} all-to-all(s16[8,9,8,128]{3,2,1,0:T(8,128)(2,1)S(1)} %get-tuple-element.8), channel_id=1, replica_groups=mesh['space'=8,'tm'=4] {'space'}, dimensions={0} | all-to-all | bytes 294912 | tf_op jit(solution)/shard_map/all_to_all | solution.py:364
  17.0 0.2 %forces.1 = (f32[2,8,256]{2,1,0:T(8,128)S(1)}, f32[3,2,8,256]{3,2,1,0:T(8,128)S(1)}, s16[13,8,128]{2,1,0:T(8,128)(2,1)S(1)}) custom-call(s16[8,9,8,128]{3,2,1,0:T(8,128)(2,1)S(1)} %all_to_all.5.parts_ref, f32[2,8,256]{2,1,0:T(8,128)S(1)} %get-tuple-element.9.atlas_ref, f32[3,2,8,256]{3,2,1,0:T(8,128)S(1)} %get-tuple-element.10.field_ref), custom_call_target="tpu_custom_call" | custom-call | tf_op jit(solution)/shard_map/forces/pallas_call | solution.py:291
  17.3 0.1 collective-permute-start.1
  17.3 0.5 %collective-permute-start = (s16[13,8,128]{2,1,0:T(8,128)(2,1)S(1)}, s16[13,8,128]{2,1,0:T(8,128)(2,1)S(1)}, u32[]{:S(2)}, u32[]{:S(2)}) collective-permute-start(s16[13,8,128]{2,1,0:T(8,128)(2,1)S(1)} %get-tuple-element.13), channel_id=1, source_target_pairs={{0,1},{1,2},{2,3},{3,0},{4,5},{5,6},{6,7},{7,4},{8,9},{9,10},{10,1... | collective-permute-start | bytes 79880 | tf_op jit(solution)/shard_map/ppermute | solution.py:332
  17.8 0.6 %copy.10 = f32[1,2,8,256]{3,2,1,0:T(8,128)} copy(f32[1,2,8,256]{3,2,1,0:T(8,128)S(1)} %bitcast.11) | data formatting | bytes 32768
  18.4 0.4 %collective-permute-done.1.after_ref = s16[13,8,128]{2,1,0:T(8,128)(2,1)S(1)} collective-permute-done((s16[13,8,128]{2,1,0:T(8,128)(2,1)S(1)}, s16[13,8,128]{2,1,0:T(8,128)(2,1)S(1)}, u32[]{:S(2)}, u32[]{:S(2)}) %collective-permute-start.1) | collective-permute-done | bytes 26656 | tf_op jit(solution)/shard_map/ppermute | solution.py:333
  18.9 2.1 %collective-permute-done.before_ref = s16[13,8,128]{2,1,0:T(8,128)(2,1)S(1)} collective-permute-done((s16[13,8,128]{2,1,0:T(8,128)(2,1)S(1)}, s16[13,8,128]{2,1,0:T(8,128)(2,1)S(1)}, u32[]{:S(2)}, u32[]{:S(2)}) %collective-permute-start) | collective-permute-done | bytes 26656 | tf_op jit(solution)/shard_map/ppermute | solution.py:332
  20.9 0.6 %smooth.1 = f32[3,2,8,256]{3,2,1,0:T(8,128)} custom-call(f32[3,2,8,256]{3,2,1,0:T(8,128)S(1)} %get-tuple-element.12.stepped_ref, s16[13,8,128]{2,1,0:T(8,128)(2,1)S(1)} %collective-permute-done.before_ref, s16[13,8,128]{2,1,0:T(8,128)(2,1)S(1)} %collective-permute-done.1.after_ref), custom_call_target="tpu_custom_call" | custom-call | tf_op jit(solution)/shard_map/smooth/pallas_call | solution.py:334
Async XLA Ops:
  17.3 1.6 %collective-permute-start.1 = (s16[13,8,128]{2,1,0:T(8,128)(2,1)S(1)}, s16[13,8,128]{2,1,0:T(8,128)(2,1)S(1)}, u32[]{:S(2)}, u32[]{:S(2)}) collective-permute-start(s16[13,8,128]{2,1,0:T(8,128)(2,1)S(1)} %get-tuple-element.13), channel_id=1, source_target_pairs={{1,0},{2,1},{3,2},{0,3},{5,4},{6,5},{7,6},{4,7},{9,8},{10,9},{11,1... | collective-permute-start | bytes 79880 | tf_op jit(solution)/shard_map/ppermute | solution.py:333
  17.3 3.6 %collective-permute-start = (s16[13,8,128]{2,1,0:T(8,128)(2,1)S(1)}, s16[13,8,128]{2,1,0:T(8,128)(2,1)S(1)}, u32[]{:S(2)}, u32[]{:S(2)}) collective-permute-start(s16[13,8,128]{2,1,0:T(8,128)(2,1)S(1)} %get-tuple-element.13), channel_id=1, source_target_pairs={{0,1},{1,2},{2,3},{3,0},{4,5},{5,6},{6,7},{7,4},{8,9},{9,10},{10,1... | collective-permute-start | bytes 79880 | tf_op jit(solution)/shard_map/ppermute | solution.py:332

commit v5 on v4

--- a/solution.py
+++ b/solution.py
@@ -39,8 +39,9 @@
     lanes = out_ref.shape[3]
     halves = length // lanes
     group = min(GROUP, bricks)
-    first = pl.program_id(0) * group
     single = bricks == group
+    first = 0 if single else pl.program_id(0) * group
+    only = (lambda when: lambda body: body()) if single else pl.when
 
     brick_ids = first + lax.broadcasted_iota(jnp.int32, (group, tiles), 0)
     by_brick = jnp.zeros((group, tiles), jnp.float32)
@@ -131,7 +132,7 @@
     tail = (layers + 2) * halves
     sums = jnp.sum(by_brick, axis=1, keepdims=True)
 
-    @pl.when(pl.program_id(0) == 0)
+    @only(pl.program_id(0) == 0)
     def _():
         atlas_out[...] = atlas_ref[...].astype(jnp.float32)
         field_out[...] = field_ref[...]
@@ -145,16 +146,17 @@
         notes_ref[brick, place : place + 1, :] = whole
         notes_ref[brick, place + 3 : place + 4, :] = rest
 
+    power, share, scale = scale_of(
+        [[total[x][b][half] for x in range(layers) for half in range(halves)] for b in range(group)]
+    )
+    weight = jnp.broadcast_to(sums * 256.0, (group, lanes)).astype(jnp.int32)
+    whole = (weight >> 8) + ((share - 64) << 9)
+    rest = (weight & 255) + ((power + 128) << 8)
     for b in range(group):
-        brick = first + b if not single else b
-        power, scale = scale_of(
-            [total[x][b][half] for x in range(layers) for half in range(halves)]
-        )
-        codes = [[coded(part, scale) for part in total[x][b]] for x in range(layers)]
-        weight = sums[b : b + 1] * 256.0
-        weight = jnp.broadcast_to(weight, (1, lanes)).astype(jnp.int32)
-        power = jnp.broadcast_to(power, (1, lanes)).astype(jnp.int32)
-        note = (weight >> 8, (weight & 255) + ((power + 128) << 8))
+        brick = first + b
+        factor = jnp.broadcast_to(scale[b : b + 1], (subs, lanes))
+        codes = [[coded(part, factor) for part in total[x][b]] for x in range(layers)]
+        note = (whole[b : b + 1], rest[b : b + 1])
 
         for x in range(layers):
             for half in range(halves):
@@ -180,7 +182,7 @@
         elif not single:
             pl.when(brick < bricks - 1)(behind)
 
-    @pl.when(pl.program_id(0) == pl.num_programs(0) - 1)
+    @only(pl.program_id(0) == pl.num_programs(0) - 1)
     def _():
         for d in range(bricks):
             out_ref[d, tail] = (notes_ref[d] - 32768).astype(jnp.int16)
@@ -221,11 +223,22 @@
     )(shift, frac, *inputs)
 
 
-def scale_of(parts):
-    largest = functools.reduce(jnp.maximum, [jnp.abs(part) for part in parts])
-    largest = jnp.max(jnp.max(largest, axis=0, keepdims=True), axis=1, keepdims=True)
-    power = jnp.floor(jnp.log2(jnp.maximum(largest, TINY))) + 1.0
-    return power, jnp.exp2(15.0 - power)
+def scale_of(blocks):
+    rows = []
+    for parts in blocks:
+        largest = functools.reduce(jnp.maximum, [jnp.abs(part) for part in parts])
+        rows.append(jnp.max(largest, axis=0, keepdims=True))
+    rows = jnp.concatenate(rows, axis=0) if len(rows) > 1 else rows[0]
+    largest = jnp.maximum(jnp.max(rows, axis=1, keepdims=True), TINY)
+    largest = jnp.broadcast_to(largest, rows.shape)
+    power = jnp.floor(jnp.log2(largest)) + 1.0
+    share = jnp.clip(jnp.ceil(largest * jnp.exp2(7.0 - power)), 64.0, 128.0)
+    scale = LIMIT * jnp.exp2(7.0 - power) / share
+    return power.astype(jnp.int32), share.astype(jnp.int32), scale
+
+
+def step_of(power, share):
+    return share.astype(jnp.float32) * jnp.exp2(power.astype(jnp.float32) - 7.0) * (1.0 / LIMIT)
 
 
 def coded(part, scale):
@@ -241,12 +254,12 @@
     numerator = [[0.0] * halves for _ in range(layers + 2)]
     for source in range(sources):
         note = parts_ref[source, slabs - 1].astype(jnp.int32) + 32768
-        wholes = wholes + note
+        wholes = wholes + (note & 511)
         rests = rests + (note & 255)
-        scale = jnp.exp2(((note >> 8) - 128).astype(jnp.float32) - 15.0)
+        steps = step_of((note[3:6] >> 8) - 128, (note[0:3] >> 9) + 64)
         for x in range(layers + 2):
-            place = 3 + min(x, 1) + (x > layers)
-            factor = jnp.broadcast_to(scale[place : place + 1], (subs, lanes))
+            place = min(x, 1) + (x > layers)
+            factor = jnp.broadcast_to(steps[place : place + 1], (subs, lanes))
             for half in range(halves):
                 code = parts_ref[source, x * halves + half].astype(jnp.int32)
                 numerator[x][half] = numerator[x][half] + code.astype(jnp.float32) * factor
@@ -280,10 +293,12 @@
             for half in range(halves):
                 part = value[:, half * lanes : (half + 1) * lanes]
                 stepped.append(((c * layers + x) * halves + half, part))
-    power, scale = scale_of([part for _, part in stepped])
+    power, share, scale = scale_of([[part for _, part in stepped]])
+    factor = jnp.broadcast_to(scale, (subs, lanes))
     for slab, part in stepped:
-        codes_ref[slab] = coded(part, scale)
-    codes_ref[len(stepped)] = jnp.broadcast_to(power, (subs, lanes)).astype(jnp.int32).astype(jnp.int16)
+        codes_ref[slab] = coded(part, factor)
+    note = power + 128 + ((share - 64) << 8)
+    codes_ref[len(stepped)] = jnp.broadcast_to(note, (subs, lanes)).astype(jnp.int16)
 
 
 def forces(parts, atlas, field):
@@ -307,10 +322,10 @@
     fields, layers, _, length = stepped_ref.shape
     slabs, _, lanes = before_ref.shape
     halves = length // lanes
-    there = [
-        (ref, jnp.exp2(ref[slabs - 1].astype(jnp.int32).astype(jnp.float32) - 15.0), inner)
-        for ref, inner in ((before_ref, at > 0), (after_ref, at < last))
-    ]
+    there = []
+    for ref, inner in ((before_ref, at > 0), (after_ref, at < last)):
+        note = ref[slabs - 1].astype(jnp.int32)
+        there.append((ref, step_of((note & 255) - 128, (note >> 8) + 64), inner))
     for c in range(fields):
         for x in range(layers):
             others = []

time: 21.8 us -> 21.8 us (level)
  no operation moved by 1% of the time
where the time goes in v5:
time: 21.8 us; the launch traced here: 21.6 us
  blocking collectives  14.6 us (67%)
  Pallas kernels  2.76 us (13%)
  waiting for transfers between devices  2.49 us (11%)
  between operations  0.66 us (3%)
  local copies, waits for them, and re-layouts  0.6 us (3%)
  starting transfers between devices  0.55 us (3%)
    all_to_all x1, blocking collectives, shards(): parts = lax.all_to_all(parts, 'space', 0, 0, tiled=True)  14.6 us
    ppermute x1, waiting for transfers between devices, smoothed(): before = lax.ppermute(codes, 'tm', forward)  2.06 us
    pallas_call x1, Pallas kernels, partial_sums(): pl.pallas_call(functools.partial(join_kernel, bricks), grid=(bricks // gr...  1.86 us
    pallas_call x1, Pallas kernels, smoothed(): pl.pallas_call(smooth_kernel, in_specs=[VMEM_SPEC, VMEM_SPEC, VMEM_SPEC],...  0.65 us
    unnamed x1, local copies, waits for them, and re-layouts  0.6 us
    ppermute x1, starting transfers between devices, smoothed(): before = lax.ppermute(codes, 'tm', forward)  0.5 us
  transfers between devices with their start and end apart: 2, of which 2 were waited for; matrix products, arithmetic and copies ran while one was open for 3% of the time, Pallas kernels for 0%

profile of v5, /device:TPU:0, one launch (start us, length us, event | category | flops | bytes accessed | tf_op | source)
XLA Modules:
  0.0 21.6 jit_solution(2380157766649207049)
XLA Ops:
  0.6 1.9 %join_tiles.1 = (s16[8,9,8,128]{3,2,1,0:T(8,128)(2,1)S(1)}, f32[2,8,256]{2,1,0:T(8,128)S(1)}, f32[3,2,8,256]{3,2,1,0:T(8,128)S(1)}) custom-call(s32[5]{0:T(128)} %shift_ref.1, bf16[1,5]{1,0:T(2,128)(2,1)} %bitcast.16, bf16[64,2,8,256]{3,2,1,0:T(8,128)(2,1)} %bitcast.12, s32[2,64]{1,0:T(2,128)} %bitcast.15, bf16[2,64]{1,0:T(2,128)(2,1)} %bitcast.17, ...), custom_call_target="tpu_custom_call" | custom-call | tf_op jit(solution)/shard_map/join_tiles/pallas_call | solution.py:211
  2.5 14.6 %all_to_all.5.parts_ref = s16[8,9,8,128]{3,2,1,0:T(8,128)(2,1)S(1)} all-to-all(s16[8,9,8,128]{3,2,1,0:T(8,128)(2,1)S(1)} %get-tuple-element.8), channel_id=1, replica_groups=mesh['space'=8,'tm'=4] {'space'}, dimensions={0} | all-to-all | bytes 294912 | tf_op jit(solution)/shard_map/all_to_all | solution.py:379
  17.1 0.2 %forces.1 = (f32[2,8,256]{2,1,0:T(8,128)S(1)}, f32[3,2,8,256]{3,2,1,0:T(8,128)S(1)}, s16[13,8,128]{2,1,0:T(8,128)(2,1)S(1)}) custom-call(s16[8,9,8,128]{3,2,1,0:T(8,128)(2,1)S(1)} %all_to_all.5.parts_ref, f32[2,8,256]{2,1,0:T(8,128)S(1)} %get-tuple-element.9.atlas_ref, f32[3,2,8,256]{3,2,1,0:T(8,128)S(1)} %get-tuple-element.10.field_ref), custom_call_target="tpu_custom_call" | custom-call | tf_op jit(solution)/shard_map/forces/pallas_call | solution.py:306
  17.3 0.1 collective-permute-start.1
  17.4 0.5 %collective-permute-start = (s16[13,8,128]{2,1,0:T(8,128)(2,1)S(1)}, s16[13,8,128]{2,1,0:T(8,128)(2,1)S(1)}, u32[]{:S(2)}, u32[]{:S(2)}) collective-permute-start(s16[13,8,128]{2,1,0:T(8,128)(2,1)S(1)} %get-tuple-element.13), channel_id=1, source_target_pairs={{0,1},{1,2},{2,3},{3,0},{4,5},{5,6},{6,7},{7,4},{8,9},{9,10},{10,1... | collective-permute-start | bytes 79880 | tf_op jit(solution)/shard_map/ppermute | solution.py:347
  17.9 0.6 %copy.10 = f32[1,2,8,256]{3,2,1,0:T(8,128)} copy(f32[1,2,8,256]{3,2,1,0:T(8,128)S(1)} %bitcast.11) | data formatting | bytes 32768
  18.5 0.4 %collective-permute-done.1.after_ref = s16[13,8,128]{2,1,0:T(8,128)(2,1)S(1)} collective-permute-done((s16[13,8,128]{2,1,0:T(8,128)(2,1)S(1)}, s16[13,8,128]{2,1,0:T(8,128)(2,1)S(1)}, u32[]{:S(2)}, u32[]{:S(2)}) %collective-permute-start.1) | collective-permute-done | bytes 26656 | tf_op jit(solution)/shard_map/ppermute | solution.py:348
  18.9 2.1 %collective-permute-done.before_ref = s16[13,8,128]{2,1,0:T(8,128)(2,1)S(1)} collective-permute-done((s16[13,8,128]{2,1,0:T(8,128)(2,1)S(1)}, s16[13,8,128]{2,1,0:T(8,128)(2,1)S(1)}, u32[]{:S(2)}, u32[]{:S(2)}) %collective-permute-start) | collective-permute-done | bytes 26656 | tf_op jit(solution)/shard_map/ppermute | solution.py:347
  21.0 0.6 %smooth.1 = f32[3,2,8,256]{3,2,1,0:T(8,128)} custom-call(f32[3,2,8,256]{3,2,1,0:T(8,128)S(1)} %get-tuple-element.12.stepped_ref, s16[13,8,128]{2,1,0:T(8,128)(2,1)S(1)} %collective-permute-done.before_ref, s16[13,8,128]{2,1,0:T(8,128)(2,1)S(1)} %collective-permute-done.1.after_ref), custom_call_target="tpu_custom_call" | custom-call | tf_op jit(solution)/shard_map/smooth/pallas_call | solution.py:349
Async XLA Ops:
  17.3 1.6 %collective-permute-start.1 = (s16[13,8,128]{2,1,0:T(8,128)(2,1)S(1)}, s16[13,8,128]{2,1,0:T(8,128)(2,1)S(1)}, u32[]{:S(2)}, u32[]{:S(2)}) collective-permute-start(s16[13,8,128]{2,1,0:T(8,128)(2,1)S(1)} %get-tuple-element.13), channel_id=1, source_target_pairs={{1,0},{2,1},{3,2},{0,3},{5,4},{6,5},{7,6},{4,7},{9,8},{10,9},{11,1... | collective-permute-start | bytes 79880 | tf_op jit(solution)/shard_map/ppermute | solution.py:348
  17.4 3.6 %collective-permute-start = (s16[13,8,128]{2,1,0:T(8,128)(2,1)S(1)}, s16[13,8,128]{2,1,0:T(8,128)(2,1)S(1)}, u32[]{:S(2)}, u32[]{:S(2)}) collective-permute-start(s16[13,8,128]{2,1,0:T(8,128)(2,1)S(1)} %get-tuple-element.13), channel_id=1, source_target_pairs={{0,1},{1,2},{2,3},{3,0},{4,5},{5,6},{6,7},{7,4},{8,9},{9,10},{10,1... | collective-permute-start | bytes 79880 | tf_op jit(solution)/shard_map/ppermute | solution.py:347

commit v6 on v5

--- a/solution.py
+++ b/solution.py
@@ -146,9 +146,15 @@
         notes_ref[brick, place : place + 1, :] = whole
         notes_ref[brick, place + 3 : place + 4, :] = rest
 
-    power, share, scale = scale_of(
-        [[total[x][b][half] for x in range(layers) for half in range(halves)] for b in range(group)]
-    )
+    largest = [
+        jnp.max(
+            largest_of([total[x][b][half] for x in range(layers) for half in range(halves)]),
+            axis=0,
+            keepdims=True,
+        )
+        for b in range(group)
+    ]
+    power, share, scale = scale_of(jnp.concatenate(largest, axis=0))
     weight = jnp.broadcast_to(sums * 256.0, (group, lanes)).astype(jnp.int32)
     whole = (weight >> 8) + ((share - 64) << 9)
     rest = (weight & 255) + ((power + 128) << 8)
@@ -223,18 +229,16 @@
     )(shift, frac, *inputs)
 
 
-def scale_of(blocks):
-    rows = []
-    for parts in blocks:
-        largest = functools.reduce(jnp.maximum, [jnp.abs(part) for part in parts])
-        rows.append(jnp.max(largest, axis=0, keepdims=True))
-    rows = jnp.concatenate(rows, axis=0) if len(rows) > 1 else rows[0]
-    largest = jnp.maximum(jnp.max(rows, axis=1, keepdims=True), TINY)
-    largest = jnp.broadcast_to(largest, rows.shape)
+def largest_of(parts):
+    return functools.reduce(jnp.maximum, [jnp.abs(part) for part in parts])
+
+
+def scale_of(largest):
+    largest = jnp.maximum(largest, TINY)
     power = jnp.floor(jnp.log2(largest)) + 1.0
-    share = jnp.clip(jnp.ceil(largest * jnp.exp2(7.0 - power)), 64.0, 128.0)
-    scale = LIMIT * jnp.exp2(7.0 - power) / share
-    return power.astype(jnp.int32), share.astype(jnp.int32), scale
+    raised = jnp.exp2(7.0 - power)
+    share = jnp.clip(jnp.ceil(largest * raised), 64.0, 128.0)
+    return power.astype(jnp.int32), share.astype(jnp.int32), LIMIT * raised / share
 
 
 def step_of(power, share):
@@ -293,12 +297,10 @@
             for half in range(halves):
                 part = value[:, half * lanes : (half + 1) * lanes]
                 stepped.append(((c * layers + x) * halves + half, part))
-    power, share, scale = scale_of([[part for _, part in stepped]])
-    factor = jnp.broadcast_to(scale, (subs, lanes))
+    power, share, scale = scale_of(largest_of([part for _, part in stepped]))
     for slab, part in stepped:
-        codes_ref[slab] = coded(part, factor)
-    note = power + 128 + ((share - 64) << 8)
-    codes_ref[len(stepped)] = jnp.broadcast_to(note, (subs, lanes)).astype(jnp.int16)
+        codes_ref[slab] = coded(part, scale)
+    codes_ref[len(stepped)] = (power + 128 + ((share - 64) << 8)).astype(jnp.int16)
 
 
 def forces(parts, atlas, field):

time: 21.8 us -> 21.6 us (level)
  no operation moved by 1% of the time
where the time goes in v6:
time: 21.6 us; the launch traced here: 21.5 us
  blocking collectives  14.6 us (68%)
  Pallas kernels  2.6 us (12%)
  waiting for transfers between devices  2.49 us (12%)
  between operations  0.66 us (3%)
  local copies, waits for them, and re-layouts  0.6 us (3%)
  starting transfers between devices  0.55 us (3%)
    all_to_all x1, blocking collectives, shards(): parts = lax.all_to_all(parts, 'space', 0, 0, tiled=True)  14.6 us
    ppermute x1, waiting for transfers between devices, smoothed(): before = lax.ppermute(codes, 'tm', forward)  2.06 us
    pallas_call x1, Pallas kernels, partial_sums(): pl.pallas_call(functools.partial(join_kernel, bricks), grid=(bricks // gr...  1.79 us
    pallas_call x1, Pallas kernels, smoothed(): pl.pallas_call(smooth_kernel, in_specs=[VMEM_SPEC, VMEM_SPEC, VMEM_SPEC],...  0.65 us
    unnamed x1, local copies, waits for them, and re-layouts  0.6 us
    ppermute x1, starting transfers between devices, smoothed(): before = lax.ppermute(codes, 'tm', forward)  0.5 us
  transfers between devices with their start and end apart: 2, of which 2 were waited for; matrix products, arithmetic and copies ran while one was open for 3% of the time, Pallas kernels for 0%

profile of v6, /device:TPU:0, one launch (start us, length us, event | category | flops | bytes accessed | tf_op | source)
XLA Modules:
  0.0 21.5 jit_solution(12987022165504468338)
XLA Ops:
  0.6 1.8 %join_tiles.1 = (s16[8,9,8,128]{3,2,1,0:T(8,128)(2,1)S(1)}, f32[2,8,256]{2,1,0:T(8,128)S(1)}, f32[3,2,8,256]{3,2,1,0:T(8,128)S(1)}) custom-call(s32[5]{0:T(128)} %shift_ref.1, bf16[1,5]{1,0:T(2,128)(2,1)} %bitcast.16, bf16[64,2,8,256]{3,2,1,0:T(8,128)(2,1)} %bitcast.12, s32[2,64]{1,0:T(2,128)} %bitcast.15, bf16[2,64]{1,0:T(2,128)(2,1)} %bitcast.17, ...), custom_call_target="tpu_custom_call" | custom-call | tf_op jit(solution)/shard_map/join_tiles/pallas_call | solution.py:217
  2.4 14.6 %all_to_all.5.parts_ref = s16[8,9,8,128]{3,2,1,0:T(8,128)(2,1)S(1)} all-to-all(s16[8,9,8,128]{3,2,1,0:T(8,128)(2,1)S(1)} %get-tuple-element.8), channel_id=1, replica_groups=mesh['space'=8,'tm'=4] {'space'}, dimensions={0} | all-to-all | bytes 294912 | tf_op jit(solution)/shard_map/all_to_all | solution.py:381
  17.0 0.2 forces.1
  17.2 0.1 collective-permute-start.1
  17.2 0.5 %collective-permute-start = (s16[13,8,128]{2,1,0:T(8,128)(2,1)S(1)}, s16[13,8,128]{2,1,0:T(8,128)(2,1)S(1)}, u32[]{:S(2)}, u32[]{:S(2)}) collective-permute-start(s16[13,8,128]{2,1,0:T(8,128)(2,1)S(1)} %get-tuple-element.13), channel_id=1, source_target_pairs={{0,1},{1,2},{2,3},{3,0},{4,5},{5,6},{6,7},{7,4},{8,9},{9,10},{10,1... | collective-permute-start | bytes 79880 | tf_op jit(solution)/shard_map/ppermute | solution.py:349
  17.7 0.6 %copy.10 = f32[1,2,8,256]{3,2,1,0:T(8,128)} copy(f32[1,2,8,256]{3,2,1,0:T(8,128)S(1)} %bitcast.11) | data formatting | bytes 32768
  18.3 0.4 %collective-permute-done.1.after_ref = s16[13,8,128]{2,1,0:T(8,128)(2,1)S(1)} collective-permute-done((s16[13,8,128]{2,1,0:T(8,128)(2,1)S(1)}, s16[13,8,128]{2,1,0:T(8,128)(2,1)S(1)}, u32[]{:S(2)}, u32[]{:S(2)}) %collective-permute-start.1) | collective-permute-done | bytes 26656 | tf_op jit(solution)/shard_map/ppermute | solution.py:350
  18.8 2.1 %collective-permute-done.before_ref = s16[13,8,128]{2,1,0:T(8,128)(2,1)S(1)} collective-permute-done((s16[13,8,128]{2,1,0:T(8,128)(2,1)S(1)}, s16[13,8,128]{2,1,0:T(8,128)(2,1)S(1)}, u32[]{:S(2)}, u32[]{:S(2)}) %collective-permute-start) | collective-permute-done | bytes 26656 | tf_op jit(solution)/shard_map/ppermute | solution.py:349
  20.8 0.6 %smooth.1 = f32[3,2,8,256]{3,2,1,0:T(8,128)} custom-call(f32[3,2,8,256]{3,2,1,0:T(8,128)S(1)} %get-tuple-element.12.stepped_ref, s16[13,8,128]{2,1,0:T(8,128)(2,1)S(1)} %collective-permute-done.before_ref, s16[13,8,128]{2,1,0:T(8,128)(2,1)S(1)} %collective-permute-done.1.after_ref), custom_call_target="tpu_custom_call" | custom-call | tf_op jit(solution)/shard_map/smooth/pallas_call | solution.py:351
Async XLA Ops:
  17.2 1.6 %collective-permute-start.1 = (s16[13,8,128]{2,1,0:T(8,128)(2,1)S(1)}, s16[13,8,128]{2,1,0:T(8,128)(2,1)S(1)}, u32[]{:S(2)}, u32[]{:S(2)}) collective-permute-start(s16[13,8,128]{2,1,0:T(8,128)(2,1)S(1)} %get-tuple-element.13), channel_id=1, source_target_pairs={{1,0},{2,1},{3,2},{0,3},{5,4},{6,5},{7,6},{4,7},{9,8},{10,9},{11,1... | collective-permute-start | bytes 79880 | tf_op jit(solution)/shard_map/ppermute | solution.py:350
  17.2 3.6 %collective-permute-start = (s16[13,8,128]{2,1,0:T(8,128)(2,1)S(1)}, s16[13,8,128]{2,1,0:T(8,128)(2,1)S(1)}, u32[]{:S(2)}, u32[]{:S(2)}) collective-permute-start(s16[13,8,128]{2,1,0:T(8,128)(2,1)S(1)} %get-tuple-element.13), channel_id=1, source_target_pairs={{0,1},{1,2},{2,3},{3,0},{4,5},{5,6},{6,7},{7,4},{8,9},{9,10},{10,1... | collective-permute-start | bytes 79880 | tf_op jit(solution)/shard_map/ppermute | solution.py:349

commit v7 on v6

--- a/solution.py
+++ b/solution.py
@@ -15,6 +15,7 @@
 TINY = 1e-30
 LIMIT = 32767.0
 EMPTY = 128 << 8
+BATCH = 2
 GROUP = 8
 
 
@@ -96,28 +97,30 @@
         )
         near = [[None] * halves for _ in range(group)]
         far = [[None] * halves for _ in range(group)]
-        for v, (amount, inside, under, factors) in enumerate(turns):
-            rolled = [
-                pltpu.roll(
-                    summed[
-                        v * group * subs : (v + 1) * group * subs, half * lanes : (half + 1) * lanes
-                    ],
-                    amount,
-                    1,
-                )
-                for half in range(halves)
-            ]
-            for b in range(group):
-                pieces = [part[b * subs : (b + 1) * subs] for part in rolled]
-                for half in range(halves):
-                    other = pieces[(half + 1) % halves]
-                    if halves > 2:
-                        other = jnp.where(under, pieces[half - 1], other)
-                    turned = jnp.where(inside, pieces[half], other)
-                    for sums, factor in zip((near, far), factors[half]):
-                        value = factor * turned
-                        old = sums[b][half]
-                        sums[b][half] = value if old is None else old + value
+        for low in range(0, group, BATCH):
+            for v, (amount, inside, under, factors) in enumerate(turns):
+                top_row = (v * group + low) * subs
+                rolled = [
+                    pltpu.roll(
+                        summed[
+                            top_row : top_row + BATCH * subs, half * lanes : (half + 1) * lanes
+                        ],
+                        amount,
+                        1,
+                    )
+                    for half in range(halves)
+                ]
+                for b in range(BATCH):
+                    pieces = [part[b * subs : (b + 1) * subs] for part in rolled]
+                    for half in range(halves):
+                        other = pieces[(half + 1) % halves]
+                        if halves > 2:
+                            other = jnp.where(under, pieces[half - 1], other)
+                        turned = jnp.where(inside, pieces[half], other)
+                        for sums, factor in zip((near, far), factors[half]):
+                            value = factor * turned
+                            old = sums[low + b][half]
+                            sums[low + b][half] = value if old is None else old + value
         pieces = []
         for b in range(group):
             ahead = [pltpu.roll(part, lanes - 1, 1) for part in far[b]]

time: 21.6 us -> 21.6 us (level)
  no operation moved by 1% of the time
where the time goes in v7:
time: 21.6 us; the launch traced here: 21.5 us
  blocking collectives  14.6 us (68%)
  Pallas kernels  2.6 us (12%)
  waiting for transfers between devices  2.49 us (12%)
  between operations  0.66 us (3%)
  local copies, waits for them, and re-layouts  0.6 us (3%)
  starting transfers between devices  0.55 us (3%)
    all_to_all x1, blocking collectives, shards(): parts = lax.all_to_all(parts, 'space', 0, 0, tiled=True)  14.6 us
    ppermute x1, waiting for transfers between devices, smoothed(): before = lax.ppermute(codes, 'tm', forward)  2.06 us
    pallas_call x1, Pallas kernels, partial_sums(): pl.pallas_call(functools.partial(join_kernel, bricks), grid=(bricks // gr...  1.79 us
    pallas_call x1, Pallas kernels, smoothed(): pl.pallas_call(smooth_kernel, in_specs=[VMEM_SPEC, VMEM_SPEC, VMEM_SPEC],...  0.65 us
    unnamed x1, local copies, waits for them, and re-layouts  0.6 us
    ppermute x1, starting transfers between devices, smoothed(): before = lax.ppermute(codes, 'tm', forward)  0.5 us
  transfers between devices with their start and end apart: 2, of which 2 were waited for; matrix products, arithmetic and copies ran while one was open for 3% of the time, Pallas kernels for 0%

profile of v7, /device:TPU:0, one launch (start us, length us, event | category | flops | bytes accessed | tf_op | source)
XLA Modules:
  0.0 21.5 jit_solution(12987022165504468338)
XLA Ops:
  0.6 1.8 %join_tiles.1 = (s16[8,9,8,128]{3,2,1,0:T(8,128)(2,1)S(1)}, f32[2,8,256]{2,1,0:T(8,128)S(1)}, f32[3,2,8,256]{3,2,1,0:T(8,128)S(1)}) custom-call(s32[5]{0:T(128)} %shift_ref.1, bf16[1,5]{1,0:T(2,128)(2,1)} %bitcast.16, bf16[64,2,8,256]{3,2,1,0:T(8,128)(2,1)} %bitcast.12, s32[2,64]{1,0:T(2,128)} %bitcast.15, bf16[2,64]{1,0:T(2,128)(2,1)} %bitcast.17, ...), custom_call_target="tpu_custom_call" | custom-call | tf_op jit(solution)/shard_map/join_tiles/pallas_call | solution.py:220
  2.4 14.6 %all_to_all.5.parts_ref = s16[8,9,8,128]{3,2,1,0:T(8,128)(2,1)S(1)} all-to-all(s16[8,9,8,128]{3,2,1,0:T(8,128)(2,1)S(1)} %get-tuple-element.8), channel_id=1, replica_groups=mesh['space'=8,'tm'=4] {'space'}, dimensions={0} | all-to-all | bytes 294912 | tf_op jit(solution)/shard_map/all_to_all | solution.py:384
  17.0 0.2 forces.1
  17.2 0.1 collective-permute-start.1
  17.2 0.5 %collective-permute-start = (s16[13,8,128]{2,1,0:T(8,128)(2,1)S(1)}, s16[13,8,128]{2,1,0:T(8,128)(2,1)S(1)}, u32[]{:S(2)}, u32[]{:S(2)}) collective-permute-start(s16[13,8,128]{2,1,0:T(8,128)(2,1)S(1)} %get-tuple-element.13), channel_id=1, source_target_pairs={{0,1},{1,2},{2,3},{3,0},{4,5},{5,6},{6,7},{7,4},{8,9},{9,10},{10,1... | collective-permute-start | bytes 79880 | tf_op jit(solution)/shard_map/ppermute | solution.py:352
  17.7 0.6 %copy.10 = f32[1,2,8,256]{3,2,1,0:T(8,128)} copy(f32[1,2,8,256]{3,2,1,0:T(8,128)S(1)} %bitcast.11) | data formatting | bytes 32768
  18.3 0.4 %collective-permute-done.1.after_ref = s16[13,8,128]{2,1,0:T(8,128)(2,1)S(1)} collective-permute-done((s16[13,8,128]{2,1,0:T(8,128)(2,1)S(1)}, s16[13,8,128]{2,1,0:T(8,128)(2,1)S(1)}, u32[]{:S(2)}, u32[]{:S(2)}) %collective-permute-start.1) | collective-permute-done | bytes 26656 | tf_op jit(solution)/shard_map/ppermute | solution.py:353
  18.8 2.1 %collective-permute-done.before_ref = s16[13,8,128]{2,1,0:T(8,128)(2,1)S(1)} collective-permute-done((s16[13,8,128]{2,1,0:T(8,128)(2,1)S(1)}, s16[13,8,128]{2,1,0:T(8,128)(2,1)S(1)}, u32[]{:S(2)}, u32[]{:S(2)}) %collective-permute-start) | collective-permute-done | bytes 26656 | tf_op jit(solution)/shard_map/ppermute | solution.py:352
  20.8 0.6 %smooth.1 = f32[3,2,8,256]{3,2,1,0:T(8,128)} custom-call(f32[3,2,8,256]{3,2,1,0:T(8,128)S(1)} %get-tuple-element.12.stepped_ref, s16[13,8,128]{2,1,0:T(8,128)(2,1)S(1)} %collective-permute-done.before_ref, s16[13,8,128]{2,1,0:T(8,128)(2,1)S(1)} %collective-permute-done.1.after_ref), custom_call_target="tpu_custom_call" | custom-call | tf_op jit(solution)/shard_map/smooth/pallas_call | solution.py:354
Async XLA Ops:
  17.2 1.6 %collective-permute-start.1 = (s16[13,8,128]{2,1,0:T(8,128)(2,1)S(1)}, s16[13,8,128]{2,1,0:T(8,128)(2,1)S(1)}, u32[]{:S(2)}, u32[]{:S(2)}) collective-permute-start(s16[13,8,128]{2,1,0:T(8,128)(2,1)S(1)} %get-tuple-element.13), channel_id=1, source_target_pairs={{1,0},{2,1},{3,2},{0,3},{5,4},{6,5},{7,6},{4,7},{9,8},{10,9},{11,1... | collective-permute-start | bytes 79880 | tf_op jit(solution)/shard_map/ppermute | solution.py:353
  17.2 3.6 %collective-permute-start = (s16[13,8,128]{2,1,0:T(8,128)(2,1)S(1)}, s16[13,8,128]{2,1,0:T(8,128)(2,1)S(1)}, u32[]{:S(2)}, u32[]{:S(2)}) collective-permute-start(s16[13,8,128]{2,1,0:T(8,128)(2,1)S(1)} %get-tuple-element.13), channel_id=1, source_target_pairs={{0,1},{1,2},{2,3},{3,0},{4,5},{5,6},{6,7},{7,4},{8,9},{9,10},{10,1... | collective-permute-start | bytes 79880 | tf_op jit(solution)/shard_map/ppermute | solution.py:352

commit v8 on v7

--- a/solution.py
+++ b/solution.py
@@ -275,8 +275,8 @@
         place = min(x, 1) + (x > layers)
         weight = wholes[place : place + 1].astype(jnp.float32)
         weight = weight + rests[place + 3 : place + 4].astype(jnp.float32) * (1.0 / 256.0)
-        below = jnp.broadcast_to(1.0 + weight, (subs, lanes))
-        image.append(jnp.concatenate([part / below for part in numerator[x]], axis=1))
+        share = jnp.broadcast_to(1.0 / (1.0 + weight), (subs, lanes))
+        image.append(jnp.concatenate([part * share for part in numerator[x]], axis=1))
     sub = lax.broadcasted_iota(jnp.int32, (subs, length), 0)
     lane = lax.broadcasted_iota(jnp.int32, (subs, length), 1)
     stepped = []

time: 21.6 us -> 21.6 us (level)
  no operation moved by 1% of the time
where the time goes in v8:
time: 21.6 us; the launch traced here: 21.5 us
  blocking collectives  14.6 us (68%)
  Pallas kernels  2.6 us (12%)
  waiting for transfers between devices  2.49 us (12%)
  between operations  0.66 us (3%)
  local copies, waits for them, and re-layouts  0.6 us (3%)
  starting transfers between devices  0.55 us (3%)
    all_to_all x1, blocking collectives, shards(): parts = lax.all_to_all(parts, 'space', 0, 0, tiled=True)  14.6 us
    ppermute x1, waiting for transfers between devices, smoothed(): before = lax.ppermute(codes, 'tm', forward)  2.06 us
    pallas_call x1, Pallas kernels, partial_sums(): pl.pallas_call(functools.partial(join_kernel, bricks), grid=(bricks // gr...  1.79 us
    pallas_call x1, Pallas kernels, smoothed(): pl.pallas_call(smooth_kernel, in_specs=[VMEM_SPEC, VMEM_SPEC, VMEM_SPEC],...  0.65 us
    unnamed x1, local copies, waits for them, and re-layouts  0.6 us
    ppermute x1, starting transfers between devices, smoothed(): before = lax.ppermute(codes, 'tm', forward)  0.5 us
  transfers between devices with their start and end apart: 2, of which 2 were waited for; matrix products, arithmetic and copies ran while one was open for 3% of the time, Pallas kernels for 0%

profile of v8, /device:TPU:0, one launch (start us, length us, event | category | flops | bytes accessed | tf_op | source)
XLA Modules:
  0.0 21.5 jit_solution(9486608132499990150)
XLA Ops:
  0.6 1.8 %join_tiles.1 = (s16[8,9,8,128]{3,2,1,0:T(8,128)(2,1)S(1)}, f32[2,8,256]{2,1,0:T(8,128)S(1)}, f32[3,2,8,256]{3,2,1,0:T(8,128)S(1)}) custom-call(s32[5]{0:T(128)} %shift_ref.1, bf16[1,5]{1,0:T(2,128)(2,1)} %bitcast.16, bf16[64,2,8,256]{3,2,1,0:T(8,128)(2,1)} %bitcast.12, s32[2,64]{1,0:T(2,128)} %bitcast.15, bf16[2,64]{1,0:T(2,128)(2,1)} %bitcast.17, ...), custom_call_target="tpu_custom_call" | custom-call | tf_op jit(solution)/shard_map/join_tiles/pallas_call | solution.py:220
  2.4 14.6 %all_to_all.5.parts_ref = s16[8,9,8,128]{3,2,1,0:T(8,128)(2,1)S(1)} all-to-all(s16[8,9,8,128]{3,2,1,0:T(8,128)(2,1)S(1)} %get-tuple-element.8), channel_id=1, replica_groups=mesh['space'=8,'tm'=4] {'space'}, dimensions={0} | all-to-all | bytes 294912 | tf_op jit(solution)/shard_map/all_to_all | solution.py:384
  17.0 0.2 forces.1
  17.2 0.1 collective-permute-start.1
  17.2 0.5 %collective-permute-start = (s16[13,8,128]{2,1,0:T(8,128)(2,1)S(1)}, s16[13,8,128]{2,1,0:T(8,128)(2,1)S(1)}, u32[]{:S(2)}, u32[]{:S(2)}) collective-permute-start(s16[13,8,128]{2,1,0:T(8,128)(2,1)S(1)} %get-tuple-element.13), channel_id=1, source_target_pairs={{0,1},{1,2},{2,3},{3,0},{4,5},{5,6},{6,7},{7,4},{8,9},{9,10},{10,1... | collective-permute-start | bytes 79880 | tf_op jit(solution)/shard_map/ppermute | solution.py:352
  17.7 0.6 %copy.10 = f32[1,2,8,256]{3,2,1,0:T(8,128)} copy(f32[1,2,8,256]{3,2,1,0:T(8,128)S(1)} %bitcast.11) | data formatting | bytes 32768
  18.3 0.4 %collective-permute-done.1.after_ref = s16[13,8,128]{2,1,0:T(8,128)(2,1)S(1)} collective-permute-done((s16[13,8,128]{2,1,0:T(8,128)(2,1)S(1)}, s16[13,8,128]{2,1,0:T(8,128)(2,1)S(1)}, u32[]{:S(2)}, u32[]{:S(2)}) %collective-permute-start.1) | collective-permute-done | bytes 26656 | tf_op jit(solution)/shard_map/ppermute | solution.py:353
  18.8 2.1 %collective-permute-done.before_ref = s16[13,8,128]{2,1,0:T(8,128)(2,1)S(1)} collective-permute-done((s16[13,8,128]{2,1,0:T(8,128)(2,1)S(1)}, s16[13,8,128]{2,1,0:T(8,128)(2,1)S(1)}, u32[]{:S(2)}, u32[]{:S(2)}) %collective-permute-start) | collective-permute-done | bytes 26656 | tf_op jit(solution)/shard_map/ppermute | solution.py:352
  20.8 0.6 %smooth.1 = f32[3,2,8,256]{3,2,1,0:T(8,128)} custom-call(f32[3,2,8,256]{3,2,1,0:T(8,128)S(1)} %get-tuple-element.12.stepped_ref, s16[13,8,128]{2,1,0:T(8,128)(2,1)S(1)} %collective-permute-done.before_ref, s16[13,8,128]{2,1,0:T(8,128)(2,1)S(1)} %collective-permute-done.1.after_ref), custom_call_target="tpu_custom_call" | custom-call | tf_op jit(solution)/shard_map/smooth/pallas_call | solution.py:354
Async XLA Ops:
  17.2 1.6 %collective-permute-start.1 = (s16[13,8,128]{2,1,0:T(8,128)(2,1)S(1)}, s16[13,8,128]{2,1,0:T(8,128)(2,1)S(1)}, u32[]{:S(2)}, u32[]{:S(2)}) collective-permute-start(s16[13,8,128]{2,1,0:T(8,128)(2,1)S(1)} %get-tuple-element.13), channel_id=1, source_target_pairs={{1,0},{2,1},{3,2},{0,3},{5,4},{6,5},{7,6},{4,7},{9,8},{10,9},{11,1... | collective-permute-start | bytes 79880 | tf_op jit(solution)/shard_map/ppermute | solution.py:353
  17.2 3.6 %collective-permute-start = (s16[13,8,128]{2,1,0:T(8,128)(2,1)S(1)}, s16[13,8,128]{2,1,0:T(8,128)(2,1)S(1)}, u32[]{:S(2)}, u32[]{:S(2)}) collective-permute-start(s16[13,8,128]{2,1,0:T(8,128)(2,1)S(1)} %get-tuple-element.13), channel_id=1, source_target_pairs={{0,1},{1,2},{2,3},{3,0},{4,5},{5,6},{6,7},{7,4},{8,9},{9,10},{10,1... | collective-permute-start | bytes 79880 | tf_op jit(solution)/shard_map/ppermute | solution.py:352
